TPU v7x, 32 devices: a whole 2x2x4 slice. The times are simulated.
32 devices in a mesh: groups: 1, ex: 32 (over z, y, x, core).
Axes of the slice: x: 2, y: 2, z: 4, core: 2. Of those that a mesh axis runs over, the one named last changes fastest.
Arguments:
- residual_in: bfloat16 [2, 1024, 2048], P(None, ('groups', 'ex')), may hold values from -6 to 6
- queries: bfloat16 [2, 1024, 2048], P(None, ('groups', 'ex')), may hold values from -100 to 100
- new_entries: bfloat16 [2, 1024, 2, 256], P(None, ('groups', 'ex')), may hold values from -6 to 6
- cache_keys: bfloat16 [2, 1024, 64, 256], P(None, ('groups', 'ex')), may hold values from -4.5 to 4.5
- cache_values: bfloat16 [2, 1024, 64, 256], P(None, ('groups', 'ex')), may hold values from -6 to 6
- lengths: int32 [2, 1024], P(None, ('groups', 'ex')), may hold values from 2 to 64, as said below
- skip_flags: int32 [2, 1024], P(None, ('groups', 'ex')), may hold values 0 or 1
- expert_ids: int32 [2, 1024, 8], P(None, ('groups', 'ex')), may hold values from 0 to 31, all different within a row; in each aligned block of 32 rows (0 to 31, 32 to 63, ..., all dimensions but the last counted through in order) at most 16 rows name the same one
- gate_weights: float32 [2, 1024, 8], P(None, ('groups', 'ex')), may hold values from 0.1 to 1
- norm_gain: float32 [2048], replicated, may hold values from 0.1 to 1.9
- gate_proj: bfloat16 [32, 2048, 768], P('ex'), may hold values from -0.125 to 0.125
- up_proj: bfloat16 [32, 2048, 768], P('ex'), may hold values from -0.125 to 0.125
- down_proj: bfloat16 [32, 768, 2048], P('ex'), may hold values from -0.21875 to 0.21875
Outputs:
- layer_out: bfloat16 [2, 1024, 2048], P(None, ('groups', 'ex'))
Inputs may be any that keep to these rules, and one draw needn't show every extreme that they name: `expert_ids`: in each micro-batch, the 32 rows of one device name any one expert at most 16 times; each row names 8 different experts. `lengths`: in each micro-batch, every device's block of 32 rows holds a row of length 64.
All inputs are finite; a program needn't handle non-finite values. No bound on the sum of `skip_flags` on one device may be relied on, other than what follows from the above.
Results may differ from a plain program's by a relative error of at most 0.0065.
Values may be sent and summed in bfloat16 or wider, within the bound.
A program may use at most 128 MiB of HBM per device.

v0:
```python
import jax
import jax.numpy as jnp
from jax import lax
from jax.sharding import PartitionSpec as P

HEADS = 16
KEY_VALUE_HEADS = 2
HEAD_WIDTH = 128


def attend(queries, entries, keys, value_entries, lengths):
    token_row_count = queries.shape[0]
    cache_slot_index = keys.shape[1]
    group = HEADS // KEY_VALUE_HEADS
    scale = HEAD_WIDTH ** (-0.5)
    qvec = queries.reshape(token_row_count, KEY_VALUE_HEADS, group, HEAD_WIDTH)
    kmat = keys.reshape(token_row_count, cache_slot_index, KEY_VALUE_HEADS, HEAD_WIDTH)
    value_matrix = value_entries.reshape(
        token_row_count, cache_slot_index, KEY_VALUE_HEADS, HEAD_WIDTH
    )
    own_key = entries[:, 0].reshape(token_row_count, KEY_VALUE_HEADS, HEAD_WIDTH)
    self_value_vector = entries[:, 1].reshape(token_row_count, KEY_VALUE_HEADS, HEAD_WIDTH)
    cache_scores = (
        jnp.einsum("rkgd,rlkd->rkgl", qvec, kmat, preferred_element_type=jnp.float32) * scale
    )
    own_scores = (
        jnp.einsum("rkgd,rkd->rkg", qvec, own_key, preferred_element_type=jnp.float32) * scale
    )
    live = (jnp.arange(cache_slot_index, dtype=jnp.int32)[None, :] < lengths[:, None])[
        :, None, None, :
    ]
    cache_scores = jnp.where(live, cache_scores, -1e30)
    top = jnp.maximum(jnp.max(cache_scores, axis=-1), own_scores)
    cache_p = jnp.where(live, jnp.exp(cache_scores - top[..., None]), 0.0)
    own_p = jnp.exp(own_scores - top)
    total = jnp.sum(cache_p, axis=-1) + own_p
    cache_weight_part = (cache_p / total[..., None]).astype(jnp.bfloat16)
    self_weight_part = (own_p / total).astype(jnp.bfloat16)
    blended_output = jnp.einsum(
        "xtio,xotw->xtiw", cache_weight_part, value_matrix, preferred_element_type=jnp.float32
    )
    blended_output = blended_output + self_weight_part[..., None].astype(
        jnp.float32
    ) * self_value_vector[:, :, None, :].astype(jnp.float32)
    return blended_output.reshape(token_row_count, HEADS * HEAD_WIDTH).astype(jnp.bfloat16)


def prepare(residual, queries, entries, keys, value_entries, lengths, norm_gain):
    attended = attend(queries, entries, keys, value_entries, lengths)
    stream = residual.astype(jnp.float32) + attended.astype(jnp.float32)
    meansq = jnp.mean(stream * stream, axis=-1, keepdims=True)
    normed = (stream / jnp.sqrt(meansq + 1e-06) * norm_gain[None, :]).astype(jnp.bfloat16)
    return (stream, normed)


def route_tables(expert_ids, gate_weights, experts, capacity):
    token_row_count, topk = expert_ids.shape
    flat_ids = expert_ids.reshape(-1)
    onehot = (flat_ids[:, None] == jnp.arange(experts, dtype=jnp.int32)[None, :]).astype(jnp.int32)
    before = jnp.cumsum(onehot, axis=0) - onehot
    rank = jnp.sum(before * onehot, axis=-1)
    slot_of = (flat_ids * capacity + rank).reshape(token_row_count, topk)
    placed = slot_of[:, :, None] == jnp.arange(experts * capacity, dtype=jnp.int32)[None, None, :]
    dispatch = jnp.sum(placed.astype(jnp.float32), axis=1).astype(jnp.bfloat16)
    gates = gate_weights / jnp.sum(gate_weights, axis=-1, keepdims=True)
    combine = jnp.sum(jnp.where(placed, gates[:, :, None], 0.0), axis=1)
    return (dispatch, combine)


def expert_rows(received, gate_proj, up_proj, down_proj):
    width = received.shape[-1]
    flat = received.reshape(-1, width)
    gate = jnp.dot(flat, gate_proj[0], preferred_element_type=jnp.float32)
    upper = jnp.dot(flat, up_proj[0], preferred_element_type=jnp.float32)
    hidden = (jax.nn.silu(gate) * upper).astype(jnp.bfloat16)
    result = jnp.dot(hidden, down_proj[0], preferred_element_type=jnp.float32).astype(jnp.bfloat16)
    return result.reshape(received.shape)


def finish(residual, stream, returned, combine, skip):
    width = residual.shape[-1]
    mixture = jnp.dot(
        combine, returned.reshape(-1, width).astype(jnp.float32), precision=lax.Precision.HIGHEST
    )
    merged = (stream + mixture).astype(jnp.bfloat16)
    return jnp.where(skip[:, None] == 1, residual, merged)


def on_device(
    residual_in,
    queries,
    new_entries,
    cache_keys,
    cache_values,
    lengths,
    skip_flags,
    expert_ids,
    gate_weights,
    norm_gain,
    gate_proj,
    up_proj,
    down_proj,
):
    micro_count = residual_in.shape[0]
    token_row_count = residual_in.shape[1]
    width = residual_in.shape[2]
    topk = expert_ids.shape[2]
    experts = gate_proj.shape[0] * lax.axis_size("ex")
    capacity = token_row_count * topk * 2 // experts
    results = []
    for micro in range(micro_count):
        stream, normed = prepare(
            residual_in[micro],
            queries[micro],
            new_entries[micro],
            cache_keys[micro],
            cache_values[micro],
            lengths[micro],
            norm_gain,
        )
        dispatch, combine = route_tables(expert_ids[micro], gate_weights[micro], experts, capacity)
        buffer = jnp.einsum(
            "rs,rd->sd", dispatch, normed, preferred_element_type=jnp.float32
        ).astype(jnp.bfloat16)
        stream, buffer, combine = (stream, buffer.reshape(experts, capacity, width), combine)
        returned = lax.all_to_all(
            expert_rows(
                lax.all_to_all(buffer, "ex", split_axis=0, concat_axis=0, tiled=True),
                gate_proj,
                up_proj,
                down_proj,
            ),
            "ex",
            split_axis=0,
            concat_axis=0,
            tiled=True,
        )
        results.append(finish(residual_in[micro], stream, returned, combine, skip_flags[micro]))
    return jnp.stack(results, axis=0)


def solution(mesh):
    in_specs = (
        P(None, ("groups", "ex"), None),
        P(None, ("groups", "ex"), None),
        P(None, ("groups", "ex"), None, None),
        P(None, ("groups", "ex"), None, None),
        P(None, ("groups", "ex"), None, None),
        P(None, ("groups", "ex")),
        P(None, ("groups", "ex")),
        P(None, ("groups", "ex"), None),
        P(None, ("groups", "ex"), None),
        P(),
        P("ex", None, None),
        P("ex", None, None),
        P("ex", None, None),
    )
    out_specs = P(None, ("groups", "ex"), None)
    return jax.shard_map(
        on_device, mesh=mesh, in_specs=in_specs, out_specs=out_specs, check_vma=False
    )
```

profile of v0, /device:TPU:0, one launch (start us, length us, event | category | flops | bytes accessed | tf_op | source)
XLA Modules:
  0.0 265.1 jit_solution(9094010036433595872)
XLA Ops:
  0.0 1.4 fusion.84
  3.5 1.3 bitcast_divide_fusion.1
  5.4 3.1 %fusion.83 = (bf16[1,32,64,256]{3,2,1,0:T(8,128)(2,1)}, bf16[1,32,64,256]{3,2,1,0:T(8,128)(2,1)}) fusion(bf16[2,32,64,256]{3,2,1,0:T(8,128)(2,1)} %param.17), kind=kLoop, calls=%fused_computation.136 | loop fusion | bytes 4194304 | tf_op jit(solution)/shard_map/slice | solution.py:117
  8.6 2.2 reshape_squeeze.33
  11.5 3.1 %fusion.82 = (bf16[1,32,64,256]{3,2,1,0:T(8,128)(2,1)}, bf16[1,32,64,256]{3,2,1,0:T(8,128)(2,1)}) fusion(bf16[2,32,64,256]{3,2,1,0:T(8,128)(2,1)} %param.16), kind=kLoop, calls=%fused_computation.135 | loop fusion | bytes 4194304 | tf_op jit(solution)/shard_map/slice | solution.py:116
  14.6 2.2 reshape_squeeze.31
  19.1 2.6 fusion.85
  23.4 1.0 fusion.43
  25.8 2.1 reshape_squeeze.29
  28.9 2.2 reshape_squeeze.27
  31.1 1.6 fusion.70
  32.7 3.2 %fusion.86 = (f32[32,2,8]{2,1,0:T(2,128)}, f32[32,2,8,64]{3,2,1,0:T(8,128)}) fusion(bf16[32,2,8,128]{3,2,1,0:T(8,128)(2,1)S(1)} %bitcast.218, bf16[32,64,2,128]{3,2,1,0:T(2,128)(2,1)} %reshape_squeeze.27, pred[32,64]{1,0:T(8,128)(4,1)} %get-tuple-element.38), kind=kOutput, calls=%fused_computation.139 | convolution fusion | flops 8486400 | bytes 1314816 | tf_op jit(solution)/shard_map/rkgd,rlkd->rkgl/dot_general | solution.py:24
  37.6 1.2 fusion.42
  39.8 1.8 fusion.33
  43.1 1.0 convert_reduce_fusion
  44.1 2.1 convolution_convert_fusion
  46.3 7.4 %all-to-all-start.2 = ((bf16[32,16,2048]{2,1,0:T(8,128)(2,1)}), bf16[32,16,2048]{2,1,0:T(8,128)(2,1)}, u32[]{:S(2)}, u32[]{:S(2)}) async-start(bf16[32,16,2048]{2,1,0:T(8,128)(2,1)} %bitcast.205), calls=%async_computation.2 | async-start | bytes 4194304 | tf_op jit(solution)/shard_map/all_to_all | solution.py:128
  55.1 1.0 convert_reduce_fusion.1
  56.1 3.1 %convolution_convert_fusion.1 = bf16[512,2048]{1,0:T(8,128)(2,1)} fusion(f32[4,8,16,128]{3,2,1,0:T(8,128)} %bitcast.208, f32[2048]{0:T(1024)S(1)} %copy-done.13, f32[32]{0:T(128)S(1)} %add_sqrt_fusion.1, bf16[2,32,2048]{2,1,0:T(8,128)(2,1)S(1)} %copy-done.1, bf16[32,512]{1,0:T(8,128)(2,1)S(1)} %get-tuple-element.7), kind=kOutput, calls=%fused_computation.15 | convolution fusion | flops 68485120 | bytes 2531840 | tf_op jit(solution)/shard_map/rs,rd->sd/dot_general | solution.py:122
  59.2 43.4 %all-to-all-done.2 = bf16[32,16,2048]{2,1,0:T(8,128)(2,1)} async-done(((bf16[32,16,2048]{2,1,0:T(8,128)(2,1)}), bf16[32,16,2048]{2,1,0:T(8,128)(2,1)}, u32[]{:S(2)}, u32[]{:S(2)}) %all-to-all-start.2) | async-done | bytes 2097184 | tf_op jit(solution)/shard_map/all_to_all | solution.py:128
  102.6 4.3 %all-to-all-start = ((bf16[32,16,2048]{2,1,0:T(8,128)(2,1)}), bf16[32,16,2048]{2,1,0:T(8,128)(2,1)}, u32[]{:S(2)}, u32[]{:S(2)}) async-start(bf16[32,16,2048]{2,1,0:T(8,128)(2,1)} %bitcast.206), calls=%async_computation | async-start | bytes 4194304 | tf_op jit(solution)/shard_map/all_to_all | solution.py:128
  106.9 5.5 %fusion.8 = f32[512,768]{1,0:T(8,128)} fusion(bf16[512,2048]{1,0:T(8,128)(2,1)} %bitcast.29, bf16[1,2048,768]{2,1,0:T(8,128)(2,1)} %param.23), kind=kOutput, calls=%fused_computation.8 | convolution fusion | flops 1610612736 | bytes 6815744 | tf_op jit(solution)/shard_map/dot_general | solution.py:73
  112.4 8.3 %fusion.15 = bf16[512,2048]{1,0:T(8,128)(2,1)} fusion(bf16[1,768,2048]{2,1,0:T(8,128)(2,1)S(1)} %copy-done, f32[512,768]{1,0:T(8,128)} %fusion.8, bf16[512,2048]{1,0:T(8,128)(2,1)} %bitcast.29, bf16[1,2048,768]{2,1,0:T(8,128)(2,1)} %param.24), kind=kOutput, calls=%fused_computation.13 | convolution fusion | flops 3224633344 | bytes 12058624 | tf_op jit(solution)/shard_map/dot_general | solution.py:76
  120.7 34.9 %all-to-all-done = bf16[32,16,2048]{2,1,0:T(8,128)(2,1)} async-done(((bf16[32,16,2048]{2,1,0:T(8,128)(2,1)}), bf16[32,16,2048]{2,1,0:T(8,128)(2,1)}, u32[]{:S(2)}, u32[]{:S(2)}) %all-to-all-start) | async-done | bytes 2097184 | tf_op jit(solution)/shard_map/all_to_all | solution.py:128
  155.6 4.1 %all-to-all-start.3 = ((bf16[32,16,2048]{2,1,0:T(8,128)(2,1)}), bf16[32,16,2048]{2,1,0:T(8,128)(2,1)}, u32[]{:S(2)}, u32[]{:S(2)}) async-start(bf16[32,16,2048]{2,1,0:T(8,128)(2,1)} %bitcast.214), calls=%async_computation.3 | async-start | bytes 4194304 | tf_op jit(solution)/shard_map/all_to_all | solution.py:126
  159.7 5.5 %fusion.10 = f32[512,768]{1,0:T(8,128)} fusion(bf16[512,2048]{1,0:T(8,128)(2,1)} %bitcast.11, bf16[1,2048,768]{2,1,0:T(8,128)(2,1)} %param.23), kind=kOutput, calls=%fused_computation.10 | convolution fusion | flops 1610612736 | bytes 6815744 | tf_op jit(solution)/shard_map/dot_general | solution.py:73
  165.3 8.3 %fusion.12 = bf16[512,2048]{1,0:T(8,128)(2,1)} fusion(bf16[1,768,2048]{2,1,0:T(8,128)(2,1)S(1)} %copy-done, f32[512,768]{1,0:T(8,128)} %fusion.10, bf16[512,2048]{1,0:T(8,128)(2,1)} %bitcast.11, bf16[1,2048,768]{2,1,0:T(8,128)(2,1)} %param.24), kind=kOutput, calls=%fused_computation.12 | convolution fusion | flops 3224633344 | bytes 12058624 | tf_op jit(solution)/shard_map/dot_general | solution.py:76
  173.6 35.0 %all-to-all-done.3 = bf16[32,16,2048]{2,1,0:T(8,128)(2,1)} async-done(((bf16[32,16,2048]{2,1,0:T(8,128)(2,1)}), bf16[32,16,2048]{2,1,0:T(8,128)(2,1)}, u32[]{:S(2)}, u32[]{:S(2)}) %all-to-all-start.3) | async-done | bytes 2097184 | tf_op jit(solution)/shard_map/all_to_all | solution.py:126
  208.6 4.1 %all-to-all-start.1 = ((bf16[32,16,2048]{2,1,0:T(8,128)(2,1)}), bf16[32,16,2048]{2,1,0:T(8,128)(2,1)}, u32[]{:S(2)}, u32[]{:S(2)}) async-start(bf16[32,16,2048]{2,1,0:T(8,128)(2,1)} %bitcast.213), calls=%async_computation.1 | async-start | bytes 4194304 | tf_op jit(solution)/shard_map/all_to_all | solution.py:126
  212.8 2.7 %fusion.21 = bf16[1,32,2048]{2,1,0:T(8,128)(2,1)S(1)} fusion(f32[32,512]{1,0:T(8,128)} %get-tuple-element.10, bf16[512,2048]{1,0:T(8,128)(2,1)} %bitcast.31, f32[4,8,16,128]{3,2,1,0:T(8,128)} %bitcast.212, pred[32]{0:T(512)(128)(4,1)S(1)} %get-tuple-element.30, bf16[2,32,2048]{2,1,0:T(8,128)(2,1)S(1)} %copy-done.1), kind=kOutput, calls=%fused_computation.21 | convolution fusion | flops 402980864 | bytes 2687008 | tf_op jit(solution)/shard_map/dot_general | solution.py:82
  215.5 46.1 %all-to-all-done.1 = bf16[32,16,2048]{2,1,0:T(8,128)(2,1)} async-done(((bf16[32,16,2048]{2,1,0:T(8,128)(2,1)}), bf16[32,16,2048]{2,1,0:T(8,128)(2,1)}, u32[]{:S(2)}, u32[]{:S(2)}) %all-to-all-start.1) | async-done | bytes 2097184 | tf_op jit(solution)/shard_map/all_to_all | solution.py:126
  261.6 2.7 %fusion.23 = bf16[1,32,2048]{2,1,0:T(8,128)(2,1)S(1)} fusion(f32[32,512]{1,0:T(8,128)} %get-tuple-element.8, bf16[512,2048]{1,0:T(8,128)(2,1)} %bitcast.16, f32[4,8,16,128]{3,2,1,0:T(8,128)} %bitcast.209, pred[32]{0:T(512)(128)(4,1)S(1)} %get-tuple-element.29, bf16[2,32,2048]{2,1,0:T(8,128)(2,1)S(1)} %copy-done.1), kind=kOutput, calls=%fused_computation.23 | convolution fusion | flops 402980864 | bytes 2687008 | tf_op jit(solution)/shard_map/dot_general | solution.py:82
  (95 shorter events, 15.9 us)
Async XLA Ops:
  0.0 112.4 %copy-start = (bf16[1,768,2048]{2,1,0:T(8,128)(2,1)S(1)}, bf16[1,768,2048]{2,1,0:T(8,128)(2,1)}, u32[]{:S(2)}) copy-start(bf16[1,768,2048]{2,1,0:T(8,128)(2,1)} %param.25) | copy-start | bytes 9437188
  8.6 2.2 copy-start.6
  14.6 2.2 copy-start.18
  14.6 2.2 copy-start.9
  16.9 2.2 copy-start.7
  19.1 2.6 copy-start.12
  23.4 4.6 %copy-start.8 = (f32[32,2,8]{2,1,0:T(2,128)}, f32[32,2,8]{2,1,0:T(2,128)S(1)}, u32[]{:S(2)}) copy-start(f32[32,2,8]{2,1,0:T(2,128)S(1)} %copy.66) | copy-start | bytes 6148
  39.8 1.8 copy-start.4
  39.8 1.8 copy-start.5
  39.8 1.8 copy-start.11
  39.8 1.9 copy-start.14
  39.8 1.9 copy-start.15
  41.6 2.6 copy-start.3
  41.6 1.2 copy-start.1
  41.7 1.5 copy-start.10
  41.7 2.5 copy-start.13
  42.1 0.7 copy-start.2
  46.3 7.4 %copy-start.17 = (s32[1,32,8]{1,2,0:T(8,128)S(1)}, s32[1,32,8]{1,2,0:T(8,128)}, u32[]{:S(2)}) copy-start(s32[1,32,8]{1,2,0:T(8,128)} %get-tuple-element.27) | copy-start | bytes 3076
  46.3 8.7 %copy-start.16 = (f32[32,8]{0,1:T(8,128)S(1)}, f32[32,8]{0,1:T(8,128)}, u32[]{:S(2)}) copy-start(f32[32,8]{0,1:T(8,128)} %get-tuple-element.25) | copy-start | bytes 3076
  46.3 56.3 %all-to-all-start.2 = ((bf16[32,16,2048]{2,1,0:T(8,128)(2,1)}), bf16[32,16,2048]{2,1,0:T(8,128)(2,1)}, u32[]{:S(2)}, u32[]{:S(2)}) async-start(bf16[32,16,2048]{2,1,0:T(8,128)(2,1)} %bitcast.205), calls=%async_computation.2 | async-start | bytes 4194304 | tf_op jit(solution)/shard_map/all_to_all | solution.py:128
  102.6 53.1 %all-to-all-start = ((bf16[32,16,2048]{2,1,0:T(8,128)(2,1)}), bf16[32,16,2048]{2,1,0:T(8,128)(2,1)}, u32[]{:S(2)}, u32[]{:S(2)}) async-start(bf16[32,16,2048]{2,1,0:T(8,128)(2,1)} %bitcast.206), calls=%async_computation | async-start | bytes 4194304 | tf_op jit(solution)/shard_map/all_to_all | solution.py:128
  155.6 53.0 %all-to-all-start.3 = ((bf16[32,16,2048]{2,1,0:T(8,128)(2,1)}), bf16[32,16,2048]{2,1,0:T(8,128)(2,1)}, u32[]{:S(2)}, u32[]{:S(2)}) async-start(bf16[32,16,2048]{2,1,0:T(8,128)(2,1)} %bitcast.214), calls=%async_computation.3 | async-start | bytes 4194304 | tf_op jit(solution)/shard_map/all_to_all | solution.py:126
  208.6 4.2 %copy-start.19 = (s32[2,32]{1,0:T(2,128)S(1)}, s32[2,32]{1,0:T(2,128)}, u32[]{:S(2)}) copy-start(s32[2,32]{1,0:T(2,128)} %param.19) | copy-start | bytes 772
  208.6 53.0 %all-to-all-start.1 = ((bf16[32,16,2048]{2,1,0:T(8,128)(2,1)}), bf16[32,16,2048]{2,1,0:T(8,128)(2,1)}, u32[]{:S(2)}, u32[]{:S(2)}) async-start(bf16[32,16,2048]{2,1,0:T(8,128)(2,1)} %bitcast.213), calls=%async_computation.1 | async-start | bytes 4194304 | tf_op jit(solution)/shard_map/all_to_all | solution.py:126
where the time goes:
time: 266 us; the launch traced here: 265 us
  waiting for transfers between devices  159 us (60%)
  matrix products  48.7 us (18%)
  local copies, waits for them, and re-layouts  26.5 us (10%)
  starting transfers between devices  20 us (8%)
  other arithmetic  10.1 us (4%)
    all_to_all x2, waiting for transfers between devices, on_device(): lax.all_to_all(expert_rows(lax.all_to_all(buffer, 'ex', split_axis=0, con...  81.2 us
    all_to_all x2, waiting for transfers between devices, on_device(): lax.all_to_all(buffer, 'ex', split_axis=0, concat_axis=0, tiled=True)  78.3 us
    dot_general x2, matrix products, expert_rows(): jnp.dot(hidden, down_proj[0], preferred_element_type=jnp.float32)  16.5 us
    all_to_all x2, starting transfers between devices, on_device(): lax.all_to_all(buffer, 'ex', split_axis=0, concat_axis=0, tiled=True)  11.7 us
    dot_general x2, matrix products, expert_rows(): gate = jnp.dot(flat, gate_proj[0], preferred_element_type=jnp.float32)  11.1 us
    all_to_all x2, starting transfers between devices, on_device(): lax.all_to_all(expert_rows(lax.all_to_all(buffer, 'ex', split_axis=0, con...  8.22 us
    dot_general x2, matrix products, attend(): jnp.einsum('rkgd,rlkd->rkgl', qvec, kmat, preferred_element_type=jnp.floa...  5.78 us
    dot_general x2, matrix products, finish(): jnp.dot(combine, returned.reshape(-1, width).astype(jnp.float32), precisi...  5.45 us
  transfers between devices with their start and end apart: 4, of which 4 were waited for; matrix products, arithmetic and copies ran while one was open for 13% of the time, Pallas kernels for 0%

commit v1 on v0

--- a/solution.py
+++ b/solution.py
@@ -53,37 +53,17 @@
     return (stream, normed)
 
 
-def route_tables(expert_ids, gate_weights, experts, capacity):
-    token_row_count, topk = expert_ids.shape
-    flat_ids = expert_ids.reshape(-1)
-    onehot = (flat_ids[:, None] == jnp.arange(experts, dtype=jnp.int32)[None, :]).astype(jnp.int32)
-    before = jnp.cumsum(onehot, axis=0) - onehot
-    rank = jnp.sum(before * onehot, axis=-1)
-    slot_of = (flat_ids * capacity + rank).reshape(token_row_count, topk)
-    placed = slot_of[:, :, None] == jnp.arange(experts * capacity, dtype=jnp.int32)[None, None, :]
-    dispatch = jnp.sum(placed.astype(jnp.float32), axis=1).astype(jnp.bfloat16)
+def combine_table(expert_ids, gate_weights, experts):
     gates = gate_weights / jnp.sum(gate_weights, axis=-1, keepdims=True)
-    combine = jnp.sum(jnp.where(placed, gates[:, :, None], 0.0), axis=1)
-    return (dispatch, combine)
+    named = expert_ids[..., None] == jnp.arange(experts, dtype=jnp.int32)
+    return jnp.sum(jnp.where(named, gates[..., None], 0.0), axis=-2)
 
 
-def expert_rows(received, gate_proj, up_proj, down_proj):
-    width = received.shape[-1]
-    flat = received.reshape(-1, width)
+def expert_rows(flat, gate_proj, up_proj, down_proj):
     gate = jnp.dot(flat, gate_proj[0], preferred_element_type=jnp.float32)
     upper = jnp.dot(flat, up_proj[0], preferred_element_type=jnp.float32)
     hidden = (jax.nn.silu(gate) * upper).astype(jnp.bfloat16)
-    result = jnp.dot(hidden, down_proj[0], preferred_element_type=jnp.float32).astype(jnp.bfloat16)
-    return result.reshape(received.shape)
-
-
-def finish(residual, stream, returned, combine, skip):
-    width = residual.shape[-1]
-    mixture = jnp.dot(
-        combine, returned.reshape(-1, width).astype(jnp.float32), precision=lax.Precision.HIGHEST
-    )
-    merged = (stream + mixture).astype(jnp.bfloat16)
-    return jnp.where(skip[:, None] == 1, residual, merged)
+    return jnp.dot(hidden, down_proj[0], preferred_element_type=jnp.float32).astype(jnp.bfloat16)
 
 
 def on_device(
@@ -101,12 +81,11 @@
     up_proj,
     down_proj,
 ):
-    micro_count = residual_in.shape[0]
-    token_row_count = residual_in.shape[1]
-    width = residual_in.shape[2]
-    topk = expert_ids.shape[2]
-    experts = gate_proj.shape[0] * lax.axis_size("ex")
-    capacity = token_row_count * topk * 2 // experts
+    micro_count, rows, width = residual_in.shape
+    shards = lax.axis_size("ex")
+    experts = gate_proj.shape[0] * shards
+    table = combine_table(expert_ids, gate_weights, experts)
+    mine = lax.all_to_all(table, "ex", split_axis=2, concat_axis=1, tiled=True)
     results = []
     for micro in range(micro_count):
         stream, normed = prepare(
@@ -118,24 +97,14 @@
             lengths[micro],
             norm_gain,
         )
-        dispatch, combine = route_tables(expert_ids[micro], gate_weights[micro], experts, capacity)
-        buffer = jnp.einsum(
-            "rs,rd->sd", dispatch, normed, preferred_element_type=jnp.float32
-        ).astype(jnp.bfloat16)
-        stream, buffer, combine = (stream, buffer.reshape(experts, capacity, width), combine)
-        returned = lax.all_to_all(
-            expert_rows(
-                lax.all_to_all(buffer, "ex", split_axis=0, concat_axis=0, tiled=True),
-                gate_proj,
-                up_proj,
-                down_proj,
-            ),
-            "ex",
-            split_axis=0,
-            concat_axis=0,
-            tiled=True,
+        gathered = lax.all_gather(normed, "ex", axis=0, tiled=True)
+        out = expert_rows(gathered, gate_proj, up_proj, down_proj)
+        partial = (mine[micro] * out.astype(jnp.float32)).astype(jnp.bfloat16)
+        mixture = lax.psum_scatter(partial, "ex", scatter_dimension=0, tiled=True)
+        merged = (stream + mixture.astype(jnp.float32)).astype(jnp.bfloat16)
+        results.append(
+            jnp.where(skip_flags[micro][:, None] == 1, residual_in[micro], merged)
         )
-        results.append(finish(residual_in[micro], stream, returned, combine, skip_flags[micro]))
     return jnp.stack(results, axis=0)
 
 

time: 266 us -> 466 us (1.75)
  waiting for transfers between devices: 159 us -> 352 us
  starting transfers between devices: 20 us -> 0.3 us
  blocking collectives: 0 us -> 14.3 us
  between operations: 0.33 us -> 13.3 us
    reduce_scatter x0 -> x2, waiting for transfers between devices: none -> 260 us  [on_device(): mixture = lax.psum_scatter(partial, 'ex', scatter_dimension=0, tiled=True)]
    all_to_all x4 -> x0, waiting for transfers between devices: 159 us -> none  [the longest x2 81.2 us: on_device(): lax.all_to_all(expert_rows(lax.all_to_all(buffer, 'ex', split_axis=0, con...]
    all_gather x0 -> x2, waiting for transfers between devices: none -> 91.5 us  [on_device(): gathered = lax.all_gather(normed, 'ex', axis=0, tiled=True)]
    all_to_all x4 -> x0, starting transfers between devices: 20 us -> none  [the longest x2 11.7 us: on_device(): lax.all_to_all(buffer, 'ex', split_axis=0, concat_axis=0, tiled=True)]
    all_to_all x0 -> x1, blocking collectives: none -> 14.3 us  [on_device(): mine = lax.all_to_all(table, 'ex', split_axis=2, concat_axis=1, tiled=True)]
    dot_general x2, matrix products: 16.5 us -> 24.8 us  [expert_rows(): jnp.dot(hidden, down_proj[0], preferred_element_type=jnp.float32)]
    dot_general x6 -> x2, matrix products: 21.7 us -> 16.4 us  [expert_rows(): upper = jnp.dot(flat, up_proj[0], preferred_element_type=jnp.float32)]
  transfers between devices with their start and end apart: 4 -> 4, of which waited for: 4 -> 4; matrix products, arithmetic and copies ran while one was open for 13% -> 9% of each run, Pallas kernels for 0% -> 0%
where the time goes in v1:
time: 466 us; the launch traced here: 465 us
  waiting for transfers between devices  352 us (76%)
  matrix products  51.6 us (11%)
  local copies, waits for them, and re-layouts  27.3 us (6%)
  blocking collectives  14.3 us (3%)
  between operations  13.3 us (3%)
  other arithmetic  6.58 us (1%)
    reduce_scatter x2, waiting for transfers between devices, on_device(): mixture = lax.psum_scatter(partial, 'ex', scatter_dimension=0, tiled=True)  260 us
    all_gather x2, waiting for transfers between devices, on_device(): gathered = lax.all_gather(normed, 'ex', axis=0, tiled=True)  91.5 us
    dot_general x2, matrix products, expert_rows(): jnp.dot(hidden, down_proj[0], preferred_element_type=jnp.float32)  24.8 us
    dot_general x2, matrix products, expert_rows(): upper = jnp.dot(flat, up_proj[0], preferred_element_type=jnp.float32)  16.4 us
    all_to_all x1, blocking collectives, on_device(): mine = lax.all_to_all(table, 'ex', split_axis=2, concat_axis=1, tiled=True)  14.3 us
  transfers between devices with their start and end apart: 4, of which 4 were waited for; matrix products, arithmetic and copies ran while one was open for 9% of the time, Pallas kernels for 0%

profile of v1, /device:TPU:0, one launch (start us, length us, event | category | flops | bytes accessed | tf_op | source)
XLA Modules:
  0.0 465.2 jit_solution(1728249540020639107)
XLA Ops:
  6.5 0.8 slice_bitcast_fusion.9
  7.4 1.8 slice_bitcast_fusion.1
  9.2 3.1 fusion.54
  12.3 2.2 reshape_squeeze.29
  14.5 2.6 fusion.57
  17.1 0.8 copy.59
  17.9 1.4 slice_bitcast_fusion.5
  20.0 0.8 fusion.43
  20.8 0.8 copy.68
  23.5 1.5 slice_convert_fusion
  24.9 3.1 fusion.55
  28.0 2.2 reshape_squeeze.31
  30.2 0.9 copy.69
  31.1 2.1 reshape_squeeze.25
  33.3 1.6 fusion.42
  34.9 3.2 fusion.56
  38.1 0.8 copy.49
  38.9 0.8 copy.66
  39.8 1.2 fusion.28
  41.3 2.1 reshape_squeeze.27
  43.5 1.8 fusion.19
  46.7 0.9 multiply_convert_fusion.5
  48.9 14.3 %all_to_all.15 = f32[2,32,32]{1,0,2:T(2,128)S(1)} all-to-all(f32[2,32,32]{1,0,2:T(2,128)S(1)} %copy.57), channel_id=1, replica_groups=mesh['groups'=1,'ex'=32] {'ex'}, dimensions={2} | all-to-all | bytes 16384 | tf_op jit(solution)/shard_map/all_to_all | solution.py:88
  63.4 49.0 %all-gather.5.cloned.1.call-done = bf16[1024,2048]{1,0:T(8,128)(2,1)} async-done(((bf16[32,2048]{1,0:T(8,128)(2,1)}), bf16[1024,2048]{1,0:T(8,128)(2,1)}) %all-gather.5.cloned.1.call-update) | async-done | bytes 4194320 | tf_op jit(solution)/shard_map/all_gather | solution.py:100
  112.4 8.2 %fusion.2 = f32[1024,768]{1,0:T(8,128)} fusion(bf16[1024,2048]{1,0:T(8,128)(2,1)} %all-gather.5.cloned.1.call-done, bf16[1,2048,768]{2,1,0:T(8,128)(2,1)} %param.24), kind=kOutput, calls=%fused_computation.4 | convolution fusion | flops 3221225472 | bytes 10485760 | tf_op jit(solution)/shard_map/dot_general | solution.py:64
  120.6 12.5 %multiply_convert_fusion = bf16[1024,2048]{1,0:T(8,128)(2,1)} fusion(f32[1024]{0:T(1024)S(1)} %mul.109, bf16[1,768,2048]{2,1,0:T(8,128)(2,1)S(1)} %copy-done, f32[1024,768]{1,0:T(8,128)} %fusion.2, bf16[1024,2048]{1,0:T(8,128)(2,1)} %all-gather.5.cloned.1.call-done, bf16[1,2048,768]{2,1,0:T(8,128)(2,1)} %param.23), kind=kOutput, calls=%fused_computation | convolution fusion | flops 6455558144 | bytes 17829888 | tf_op jit(solution)/shard_map/dot_general | solution.py:66
  133.4 42.5 %all-gather.3.cloned.1.call-done = bf16[1024,2048]{1,0:T(8,128)(2,1)} async-done(((bf16[32,2048]{1,0:T(8,128)(2,1)}), bf16[1024,2048]{1,0:T(8,128)(2,1)}) %all-gather.3.cloned.1.call-update) | async-done | bytes 4194320 | tf_op jit(solution)/shard_map/all_gather | solution.py:100
  175.9 8.2 %fusion.4 = f32[1024,768]{1,0:T(8,128)} fusion(bf16[1024,2048]{1,0:T(8,128)(2,1)} %all-gather.3.cloned.1.call-done, bf16[1,2048,768]{2,1,0:T(8,128)(2,1)} %param.24), kind=kOutput, calls=%fused_computation.6 | convolution fusion | flops 3221225472 | bytes 10485760 | tf_op jit(solution)/shard_map/dot_general | solution.py:64
  184.1 12.3 %multiply_convert_fusion.1 = bf16[1024,2048]{1,0:T(8,128)(2,1)} fusion(f32[1024]{0:T(1024)S(1)} %mul.96, bf16[1,768,2048]{2,1,0:T(8,128)(2,1)S(1)} %copy-done, f32[1024,768]{1,0:T(8,128)} %fusion.4, bf16[1024,2048]{1,0:T(8,128)(2,1)} %all-gather.3.cloned.1.call-done, bf16[1,2048,768]{2,1,0:T(8,128)(2,1)} %param.23), kind=kOutput, calls=%fused_computation.1 | convolution fusion | flops 6455558144 | bytes 17829888 | tf_op jit(solution)/shard_map/dot_general | solution.py:66
  197.1 120.5 %reduce-scatter.5.cloned.1.call-done = bf16[32,2048]{1,0:T(8,128)(2,1)} async-done(((bf16[1024,2048]{1,0:T(8,128)(2,1)}), bf16[32,2048]{1,0:T(8,128)(2,1)}) %reduce-scatter.5.cloned.1.call-update) | async-done | bytes 131088 | tf_op jit(solution)/shard_map/reduce_scatter | solution.py:103
  317.6 139.0 %reduce-scatter.3.cloned.1.call-done = bf16[32,2048]{1,0:T(8,128)(2,1)} async-done(((bf16[1024,2048]{1,0:T(8,128)(2,1)}), bf16[32,2048]{1,0:T(8,128)(2,1)}) %reduce-scatter.3.cloned.1.call-update) | async-done | bytes 131088 | tf_op jit(solution)/shard_map/reduce_scatter | solution.py:103
  456.6 2.1 fusion.31
  (64 shorter events, 6.6 us)
Async XLA Ops:
  6.5 114.1 %copy-start = (bf16[1,768,2048]{2,1,0:T(8,128)(2,1)S(1)}, bf16[1,768,2048]{2,1,0:T(8,128)(2,1)}, u32[]{:S(2)}) copy-start(bf16[1,768,2048]{2,1,0:T(8,128)(2,1)} %param.25) | copy-start | bytes 9437188
  6.5 105.9 %all-gather.5.cloned.1.call-start = ((), (), s32[]{:S(2)}) async-start(), calls=%async_computation.5 | async-start | bytes 4325376 | tf_op jit(solution)/shard_map/all_gather | solution.py:100
  19.4 0.6 copy-start.6
  21.7 8.5 %copy-start.7 = (f32[32,2,8]{2,1,0:T(2,128)}, f32[32,2,8]{2,1,0:T(2,128)S(1)}, u32[]{:S(2)}) copy-start(f32[32,2,8]{2,1,0:T(2,128)S(1)} %copy.60) | copy-start | bytes 6148
  43.5 1.9 copy-start.4
  43.5 1.9 copy-start.5
  43.5 1.9 copy-start.9
  45.3 1.3 copy-start.2
  45.3 1.0 copy-start.1
  45.4 1.3 copy-start.10
  45.4 3.0 copy-start.8
  45.4 3.1 copy-start.11
  45.8 1.7 copy-start.3
  47.6 128.3 %all-gather.3.cloned.1.call-start = ((), (), s32[]{:S(2)}) async-start(), calls=%async_computation.3 | async-start | bytes 4325376 | tf_op jit(solution)/shard_map/all_gather | solution.py:100
  48.3 269.3 %reduce-scatter.5.cloned.1.call-start = ((), (), s32[]{:S(2)}) async-start(), calls=%async_computation.6 | async-start | bytes 4325376 | tf_op jit(solution)/shard_map/reduce_scatter | solution.py:103
  133.1 323.5 %reduce-scatter.3.cloned.1.call-start = ((), (), s32[]{:S(2)}) async-start(), calls=%async_computation.4 | async-start | bytes 4325376 | tf_op jit(solution)/shard_map/reduce_scatter | solution.py:103
  196.4 0.7 copy-start.12
Sparse Core Ops, SparseCore 0:
  47.7 64.6 all-gather.4
  115.3 60.5 all-gather.2
  178.2 139.4 reduce-scatter.4
  319.8 136.7 reduce-scatter.2

commit v2 on v1

v2 whole, which is shorter than its diff:
```python
import jax
import jax.numpy as jnp
from jax import lax
from jax.experimental import pallas as pl
from jax.experimental.pallas import tpu as pltpu
from jax.sharding import PartitionSpec as P

HEADS = 16
KEY_VALUE_HEADS = 2
HEAD_WIDTH = 128
ROW_BLOCK = 16


def attend_kernel(len_ref, q_ref, e_ref, k_ref, v_ref, o_ref):
    rows, heads, width = q_ref.shape[1:]
    slots = k_ref.shape[2]
    scale = HEAD_WIDTH ** (-0.5)
    q = q_ref[0]
    entries = e_ref[0]
    group = heads // KEY_VALUE_HEADS
    which = lax.broadcasted_iota(jnp.int32, (rows, heads, width), 1) // group
    zero = jnp.zeros_like(q)
    wide = jnp.concatenate(
        [jnp.where(which == g, q, zero) for g in range(KEY_VALUE_HEADS)], axis=-1
    )
    scores = (
        jnp.einsum("rhd,rld->rhl", wide, k_ref[0], preferred_element_type=jnp.float32) * scale
    )
    own = (
        jnp.sum(
            wide.astype(jnp.float32) * entries[:, 0:1, :].astype(jnp.float32),
            axis=-1,
            keepdims=True,
        )
        * scale
    )
    live = lax.broadcasted_iota(jnp.int32, (rows, heads, slots), 2) < len_ref[0]
    scores = jnp.where(live, scores, -1e30)
    top = jnp.maximum(jnp.max(scores, axis=-1, keepdims=True), own)
    p = jnp.where(live, jnp.exp(scores - top), 0.0)
    own_p = jnp.exp(own - top)
    total = jnp.sum(p, axis=-1, keepdims=True) + own_p
    weights = (p / total).astype(jnp.bfloat16)
    own_w = (own_p / total).astype(jnp.bfloat16).astype(jnp.float32)
    out = jnp.einsum("rhl,rld->rhd", weights, v_ref[0], preferred_element_type=jnp.float32)
    out = out + own_w * entries[:, 1:2, :].astype(jnp.float32)
    result = out[..., :width]
    for g in range(1, KEY_VALUE_HEADS):
        result = jnp.where(which == g, out[..., g * width : (g + 1) * width], result)
    o_ref[...] = result.astype(jnp.bfloat16)


def attend(micro, queries, entries, keys, values, lengths):
    rows, slots, kv_width = keys.shape[1:]
    block = ROW_BLOCK if rows % ROW_BLOCK == 0 else rows
    return pl.pallas_call(
        attend_kernel,
        out_shape=jax.ShapeDtypeStruct((rows, HEADS, HEAD_WIDTH), jnp.bfloat16),
        grid=(rows // block,),
        in_specs=[
            pl.BlockSpec((1, block, 1, 1), lambda i: (micro, i, 0, 0)),
            pl.BlockSpec((1, block, HEADS, HEAD_WIDTH), lambda i: (micro, i, 0, 0)),
            pl.BlockSpec((1, block, 2, kv_width), lambda i: (micro, i, 0, 0)),
            pl.BlockSpec((1, block, slots, kv_width), lambda i: (micro, i, 0, 0)),
            pl.BlockSpec((1, block, slots, kv_width), lambda i: (micro, i, 0, 0)),
        ],
        out_specs=pl.BlockSpec((block, HEADS, HEAD_WIDTH), lambda i: (i, 0, 0)),
        compiler_params=pltpu.CompilerParams(vmem_limit_bytes=32 << 20),
        cost_estimate=pl.CostEstimate(
            flops=rows * HEADS * slots * kv_width * 4,
            bytes_accessed=rows * slots * kv_width * 4,
            transcendentals=rows * HEADS * slots,
        ),
    )(lengths, queries, entries, keys, values)


def combine_table(expert_ids, gate_weights, experts):
    gates = gate_weights / jnp.sum(gate_weights, axis=-1, keepdims=True)
    named = expert_ids[..., None] == jnp.arange(experts, dtype=jnp.int32)
    return jnp.sum(jnp.where(named, gates[..., None], 0.0), axis=-2)


def swap(x, bit, shards):
    return lax.ppermute(x, "ex", [(i, i ^ (1 << bit)) for i in range(shards)])


def weighted_rows(flat, weight, gate_proj, up_proj, down_proj):
    gate = jnp.dot(flat, gate_proj[0], preferred_element_type=jnp.float32)
    upper = jnp.dot(flat, up_proj[0], preferred_element_type=jnp.float32)
    hidden = (jax.nn.silu(gate) * upper).astype(jnp.bfloat16)
    out = jnp.dot(hidden, down_proj[0], preferred_element_type=jnp.float32)
    out = out.astype(jnp.bfloat16).astype(jnp.float32)
    return (weight * out).astype(jnp.bfloat16)


def wide_sum(a, b):
    return (a.astype(jnp.float32) + b.astype(jnp.float32)).astype(jnp.bfloat16)


def on_device(
    residual_in,
    queries,
    new_entries,
    cache_keys,
    cache_values,
    lengths,
    skip_flags,
    expert_ids,
    gate_weights,
    norm_gain,
    gate_proj,
    up_proj,
    down_proj,
):
    micro_count, rows, width = residual_in.shape
    shards = lax.axis_size("ex")
    bits = shards.bit_length() - 1
    experts = gate_proj.shape[0] * shards
    table = combine_table(expert_ids, gate_weights, experts)
    mine = lax.all_to_all(table, "ex", split_axis=2, concat_axis=1, tiled=True)
    mine = mine.reshape(micro_count, shards, rows)
    me = lax.axis_index("ex")
    down = list(range(bits - 1, -1, -1))
    other = down[:-3] + [down[-2], down[-3], down[-1]] if bits >= 3 else down
    orders = (down, other)
    half = rows // 2
    queries = queries.reshape(micro_count, rows, HEADS, HEAD_WIDTH)
    lengths = lengths.reshape(micro_count, rows, 1, 1)
    streams = []
    parts = []
    for micro in range(micro_count):
        attended = attend(micro, queries, new_entries, cache_keys, cache_values, lengths)
        stream = residual_in[micro].astype(jnp.float32) + attended.reshape(rows, width).astype(
            jnp.float32
        )
        meansq = jnp.mean(stream * stream, axis=-1, keepdims=True)
        normed = (stream / jnp.sqrt(meansq + 1e-06) * norm_gain[None, :]).astype(jnp.bfloat16)
        streams.append(stream)
        for side, order in enumerate(orders):
            parts.append((micro, side, order, normed[side * half : (side + 1) * half]))
    sums = {}
    for micro, side, order, buf in parts:
        spread = [0]
        for bit in order:
            spread = spread + [k ^ (1 << bit) for k in spread]
        weight = jnp.take(
            mine[micro, :, side * half : (side + 1) * half],
            jnp.bitwise_xor(me, jnp.array(spread, dtype=jnp.int32)),
            axis=0,
        ).reshape(2, -1, 1)
        for bit in order[:-1]:
            buf = jnp.concatenate([buf, swap(buf, bit, shards)], axis=0)
        far = swap(buf, order[-1], shards)
        back = swap(
            weighted_rows(far, weight[1], gate_proj, up_proj, down_proj), order[-1], shards
        )
        acc = wide_sum(weighted_rows(buf, weight[0], gate_proj, up_proj, down_proj), back)
        for bit in order[-2::-1]:
            keep = acc.shape[0] // 2
            acc = wide_sum(acc[:keep], swap(acc[keep:], bit, shards))
        sums[micro, side] = acc
    results = []
    for micro in range(micro_count):
        mixture = jnp.concatenate([sums[micro, 0], sums[micro, 1]], axis=0)
        merged = (streams[micro] + mixture.astype(jnp.float32)).astype(jnp.bfloat16)
        results.append(jnp.where(skip_flags[micro][:, None] == 1, residual_in[micro], merged))
    return jnp.stack(results, axis=0)


def solution(mesh):
    in_specs = (
        P(None, ("groups", "ex"), None),
        P(None, ("groups", "ex"), None),
        P(None, ("groups", "ex"), None, None),
        P(None, ("groups", "ex"), None, None),
        P(None, ("groups", "ex"), None, None),
        P(None, ("groups", "ex")),
        P(None, ("groups", "ex")),
        P(None, ("groups", "ex"), None),
        P(None, ("groups", "ex"), None),
        P(),
        P("ex", None, None),
        P("ex", None, None),
        P("ex", None, None),
    )
    out_specs = P(None, ("groups", "ex"), None)
    return jax.shard_map(
        on_device, mesh=mesh, in_specs=in_specs, out_specs=out_specs, check_vma=False
    )
```

time: 466 us -> 213 us (0.46)
  waiting for transfers between devices: 352 us -> 39.9 us
  starting transfers between devices: 0.3 us -> 43.4 us
  matrix products: 51.6 us -> 70.9 us
  blocking collectives: 14.3 us -> 0 us
  between operations: 13.3 us -> 0.65 us
  other arithmetic: 6.58 us -> 16.9 us
  local copies, waits for them, and re-layouts: 27.3 us -> 37.3 us
    reduce_scatter x2 -> x0, waiting for transfers between devices: 260 us -> none  [on_device(): mixture = lax.psum_scatter(partial, 'ex', scatter_dimension=0, tiled=True)]
    all_gather x2 -> x0, waiting for transfers between devices: 91.5 us -> none  [on_device(): gathered = lax.all_gather(normed, 'ex', axis=0, tiled=True)]
    ppermute x0 -> x40, waiting for transfers between devices: none -> 39.9 us  [swap(): return lax.ppermute(x, 'ex', [(i, i ^ 1 << bit) for i in range(shards)])]
    ppermute x0 -> x40, starting transfers between devices: none -> 39.5 us  [swap(): return lax.ppermute(x, 'ex', [(i, i ^ 1 << bit) for i in range(shards)])]
    dot_general x10 -> x16, matrix products: 51.6 us -> 70.9 us  [the longest x8 45.5 us: weighted_rows(): out = jnp.dot(hidden, down_proj[0], preferred_element_type=jnp.float32)]
    unnamed x30 -> x70, local copies, waits for them, and re-layouts: 4.6 us -> 19.1 us
    all_to_all x1 -> x0, blocking collectives: 14.3 us -> none  [on_device(): mine = lax.all_to_all(table, 'ex', split_axis=2, concat_axis=1, tiled=True)]
    concatenate x0 -> x16, other arithmetic: none -> 10.8 us  [the longest x12 10.7 us: on_device(): buf = jnp.concatenate([buf, swap(buf, bit, shards)], axis=0)]
  transfers between devices with their start and end apart: 4 -> 41, of which waited for: 4 -> 12; matrix products, arithmetic and copies ran while one was open for 9% -> 54% of each run, Pallas kernels for 0% -> 0%
where the time goes in v2:
time: 213 us; the launch traced here: 211 us
  matrix products  70.9 us (33%)
  starting transfers between devices  43.4 us (20%)
  waiting for transfers between devices  39.9 us (19%)
  local copies, waits for them, and re-layouts  37.3 us (18%)
  other arithmetic  16.9 us (8%)
  Pallas kernels  2.19 us (1%)
    dot_general x8, matrix products, weighted_rows(): out = jnp.dot(hidden, down_proj[0], preferred_element_type=jnp.float32)  45.5 us
    ppermute x40, waiting for transfers between devices, swap(): return lax.ppermute(x, 'ex', [(i, i ^ 1 << bit) for i in range(shards)])  39.9 us
    ppermute x40, starting transfers between devices, swap(): return lax.ppermute(x, 'ex', [(i, i ^ 1 << bit) for i in range(shards)])  39.5 us
    dot_general x8, matrix products, weighted_rows(): upper = jnp.dot(flat, up_proj[0], preferred_element_type=jnp.float32)  25.4 us
    unnamed x70, local copies, waits for them, and re-layouts  19.1 us
    concatenate x12, other arithmetic, on_device(): buf = jnp.concatenate([buf, swap(buf, bit, shards)], axis=0)  10.7 us
    slice x16, local copies, waits for them, and re-layouts, on_device(): acc = wide_sum(acc[:keep], swap(acc[keep:], bit, shards))  6.99 us
    convert_element_type x12, other arithmetic, wide_sum(): return (a.astype(jnp.float32) + b.astype(jnp.float32)).astype(jnp.bfloat16)  4.4 us
  transfers between devices with their start and end apart: 41, of which 12 were waited for; matrix products, arithmetic and copies ran while one was open for 54% of the time, Pallas kernels for 0%

profile of v2, /device:TPU:0, one launch (start us, length us, event | category | flops | bytes accessed | tf_op | source)
XLA Modules:
  0.0 211.3 jit_solution(10178027064484580516)
XLA Ops:
  10.9 4.0 %collective-permute-start.20 = (bf16[16,2048]{1,0:T(8,128)(2,1)}, bf16[16,2048]{1,0:T(8,128)(2,1)}, u32[]{:S(2)}, u32[]{:S(2)}) collective-permute-start(bf16[16,2048]{1,0:T(8,128)(2,1)} %get-tuple-element.20), channel_id=1, source_target_pairs={{0,16},{1,17},{2,18},{3,19},{4,20},{5,21},{6,22},{7,23},{8,24},{9,... | collective-permute-start | bytes 196616 | tf_op jit(solution)/shard_map/ppermute | solution.py:84
  16.0 4.0 %all-to-all-start = ((f32[2,32,32]{1,0,2:T(2,128)}), f32[2,32,32]{1,0,2:T(2,128)}, u32[]{:S(2)}, u32[]{:S(2)}) async-start(f32[2,32,32]{1,0,2:T(2,128)} %copy.30), calls=%async_computation | async-start | bytes 65536 | tf_op jit(solution)/shard_map/all_to_all | solution.py:120
  20.0 2.7 %collective-permute-start.30 = (bf16[16,2048]{1,0:T(8,128)(2,1)}, bf16[16,2048]{1,0:T(8,128)(2,1)}, u32[]{:S(2)}, u32[]{:S(2)}) collective-permute-start(bf16[16,2048]{1,0:T(8,128)(2,1)} %get-tuple-element.23), channel_id=1, source_target_pairs={{0,16},{1,17},{2,18},{3,19},{4,20},{5,21},{6,22},{7,23},{8,24},{9,... | collective-permute-start | bytes 196616 | tf_op jit(solution)/shard_map/ppermute | solution.py:84
  23.7 2.6 %collective-permute-start.10 = (bf16[16,2048]{1,0:T(8,128)(2,1)}, bf16[16,2048]{1,0:T(8,128)(2,1)}, u32[]{:S(2)}, u32[]{:S(2)}) collective-permute-start(bf16[16,2048]{1,0:T(8,128)(2,1)} %get-tuple-element.19), channel_id=1, source_target_pairs={{0,16},{1,17},{2,18},{3,19},{4,20},{5,21},{6,22},{7,23},{8,24},{9,... | collective-permute-start | bytes 196616 | tf_op jit(solution)/shard_map/ppermute | solution.py:84
  67.7 7.8 %collective-permute-done.23 = bf16[128,2048]{1,0:T(8,128)(2,1)S(1)} collective-permute-done((bf16[128,2048]{1,0:T(8,128)(2,1)S(1)}, bf16[128,2048]{1,0:T(8,128)(2,1)S(1)}, u32[]{:S(2)}, u32[]{:S(2)}) %collective-permute-start.23) | collective-permute-done | bytes 524320 | tf_op jit(solution)/shard_map/ppermute | solution.py:84
  77.0 7.2 %collective-permute-done.3 = bf16[128,2048]{1,0:T(8,128)(2,1)S(1)} collective-permute-done((bf16[128,2048]{1,0:T(8,128)(2,1)S(1)}, bf16[128,2048]{1,0:T(8,128)(2,1)S(1)}, u32[]{:S(2)}, u32[]{:S(2)}) %collective-permute-start.3) | collective-permute-done | bytes 524320 | tf_op jit(solution)/shard_map/ppermute | solution.py:84
  85.1 1.9 fusion.22
  88.3 3.1 %fusion.18 = f32[256,768]{1,0:T(8,128)} fusion(bf16[256,2048]{1,0:T(8,128)(2,1)} %constant_dynamic-update-slice_fusion.15, bf16[1,2048,768]{2,1,0:T(8,128)(2,1)S(1)} %copy-done.24), kind=kOutput, calls=%fused_computation.22 | convolution fusion | flops 805306368 | bytes 4980736 | tf_op jit(solution)/shard_map/dot_general | solution.py:89
  91.4 3.1 %fusion.30 = f32[256,768]{1,0:T(8,128)} fusion(bf16[256,2048]{1,0:T(8,128)(2,1)} %constant_dynamic-update-slice_fusion, bf16[1,2048,768]{2,1,0:T(8,128)(2,1)S(1)} %copy-done.24), kind=kOutput, calls=%fused_computation.34 | convolution fusion | flops 805306368 | bytes 4980736 | tf_op jit(solution)/shard_map/dot_general | solution.py:89
  94.5 3.1 %fusion.26 = f32[256,768]{1,0:T(8,128)} fusion(bf16[256,2048]{1,0:T(8,128)(2,1)} %constant_dynamic-update-slice_fusion.5, bf16[1,2048,768]{2,1,0:T(8,128)(2,1)S(1)} %copy-done.24), kind=kOutput, calls=%fused_computation.30 | convolution fusion | flops 805306368 | bytes 4980736 | tf_op jit(solution)/shard_map/dot_general | solution.py:89
  98.5 1.9 fusion.20
  100.4 5.6 %fusion.126 = bf16[256,2048]{1,0:T(8,128)(2,1)} fusion(bf16[1,768,2048]{2,1,0:T(8,128)(2,1)S(1)} %copy-done, f32[256]{0:T(256)S(1)} %mul.179, f32[256,768]{1,0:T(8,128)} %fusion.20, bf16[256,2048]{1,0:T(8,128)(2,1)} %copy-done.25, bf16[1,2048,768]{2,1,0:T(8,128)(2,1)} %param.29), kind=kOutput, calls=%fused_computation.78 | convolution fusion | flops 1613889536 | bytes 9176064 | tf_op jit(solution)/shard_map/dot_general | solution.py:91
  106.0 4.1 %fusion.16 = f32[256,768]{1,0:T(8,128)} fusion(bf16[256,2048]{1,0:T(8,128)(2,1)} %collective-permute-done.34, bf16[1,2048,768]{2,1,0:T(8,128)(2,1)} %param.30), kind=kOutput, calls=%fused_computation.20 | convolution fusion | flops 805306368 | bytes 4980736 | tf_op jit(solution)/shard_map/dot_general | solution.py:89
  110.1 5.5 %fusion.153 = bf16[256,2048]{1,0:T(8,128)(2,1)} fusion(bf16[1,768,2048]{2,1,0:T(8,128)(2,1)S(1)} %copy-done, f32[256]{0:T(256)S(1)} %mul.189, f32[256,768]{1,0:T(8,128)} %fusion.16, bf16[256,2048]{1,0:T(8,128)(2,1)} %collective-permute-done.34, bf16[1,2048,768]{2,1,0:T(8,128)(2,1)} %param.29), kind=kOutput, calls=%fused_computation.87 | convolution fusion | flops 1613889536 | bytes 9176064 | tf_op jit(solution)/shard_map/dot_general | solution.py:91
  116.1 4.2 %fusion.28 = f32[256,768]{1,0:T(8,128)} fusion(bf16[256,2048]{1,0:T(8,128)(2,1)} %collective-permute-done.4, bf16[1,2048,768]{2,1,0:T(8,128)(2,1)} %param.30), kind=kOutput, calls=%fused_computation.32 | convolution fusion | flops 805306368 | bytes 4980736 | tf_op jit(solution)/shard_map/dot_general | solution.py:89
  120.3 5.5 %fusion.72 = bf16[256,2048]{1,0:T(8,128)(2,1)} fusion(bf16[1,768,2048]{2,1,0:T(8,128)(2,1)S(1)} %copy-done, f32[256]{0:T(256)S(1)} %mul.157, f32[256,768]{1,0:T(8,128)} %fusion.28, bf16[256,2048]{1,0:T(8,128)(2,1)} %collective-permute-done.4, bf16[1,2048,768]{2,1,0:T(8,128)(2,1)} %param.29), kind=kOutput, calls=%fused_computation.60 | convolution fusion | flops 1613889536 | bytes 9176064 | tf_op jit(solution)/shard_map/dot_general | solution.py:91
  125.9 4.1 %fusion.24 = f32[256,768]{1,0:T(8,128)} fusion(bf16[256,2048]{1,0:T(8,128)(2,1)} %collective-permute-done.14, bf16[1,2048,768]{2,1,0:T(8,128)(2,1)} %param.30), kind=kOutput, calls=%fused_computation.28 | convolution fusion | flops 805306368 | bytes 4980736 | tf_op jit(solution)/shard_map/dot_general | solution.py:89
  129.9 5.5 %fusion.99 = bf16[256,2048]{1,0:T(8,128)(2,1)} fusion(bf16[1,768,2048]{2,1,0:T(8,128)(2,1)S(1)} %copy-done, f32[256]{0:T(256)S(1)} %mul.167, f32[256,768]{1,0:T(8,128)} %fusion.24, bf16[256,2048]{1,0:T(8,128)(2,1)} %collective-permute-done.14, bf16[1,2048,768]{2,1,0:T(8,128)(2,1)} %param.29), kind=kOutput, calls=%fused_computation.69 | convolution fusion | flops 1613889536 | bytes 9176064 | tf_op jit(solution)/shard_map/dot_general | solution.py:91
  135.9 5.9 %add_convert_fusion.1 = bf16[256,2048]{1,0:T(8,128)(2,1)} fusion(bf16[256,2048]{1,0:T(8,128)(2,1)} %collective-permute-done.25, bf16[1,768,2048]{2,1,0:T(8,128)(2,1)S(1)} %copy-done, f32[256]{0:T(256)S(1)} %mul.172, f32[256,768]{1,0:T(8,128)} %fusion.22, bf16[256,2048]{1,0:T(8,128)(2,1)} %copy-done.18, bf16[1,2048,768]{2,1,0:T(8,128)(2,1)} %param.29), kind=kOutput, calls=%fused_computation.89 | convolution fusion | flops 1615986688 | bytes 10224640 | tf_op jit(solution)/shard_map/dot_general | solution.py:91
  141.8 1.9 slice.255
  144.9 5.9 %add_convert_fusion = bf16[256,2048]{1,0:T(8,128)(2,1)} fusion(bf16[256,2048]{1,0:T(8,128)(2,1)} %collective-permute-done.35, bf16[1,768,2048]{2,1,0:T(8,128)(2,1)S(1)} %copy-done, f32[256]{0:T(256)S(1)} %mul.184, f32[256,768]{1,0:T(8,128)} %fusion.18, bf16[256,2048]{1,0:T(8,128)(2,1)} %constant_dynamic-update-slice_fusion.15, bf16[1,2048,768]{2,1,0:T(8,128)(2,1)} %param.29), kind=kOutput, calls=%fused_computation.88 | convolution fusion | flops 1615986688 | bytes 10224640 | tf_op jit(solution)/shard_map/dot_general | solution.py:91
  150.8 1.9 slice.267
  153.5 5.9 %add_convert_fusion.3 = bf16[256,2048]{1,0:T(8,128)(2,1)} fusion(bf16[256,2048]{1,0:T(8,128)(2,1)} %collective-permute-done.5, bf16[1,768,2048]{2,1,0:T(8,128)(2,1)S(1)} %copy-done, f32[256]{0:T(256)S(1)} %mul.149, f32[256,768]{1,0:T(8,128)} %fusion.30, bf16[256,2048]{1,0:T(8,128)(2,1)} %constant_dynamic-update-slice_fusion, bf16[1,2048,768]{2,1,0:T(8,128)(2,1)} %param.29), kind=kOutput, calls=%fused_computation.91 | convolution fusion | flops 1615986688 | bytes 10224640 | tf_op jit(solution)/shard_map/dot_general | solution.py:91
  159.3 1.9 slice.231
  161.8 5.8 %add_convert_fusion.2 = bf16[256,2048]{1,0:T(8,128)(2,1)} fusion(bf16[256,2048]{1,0:T(8,128)(2,1)} %collective-permute-done.15, bf16[1,768,2048]{2,1,0:T(8,128)(2,1)S(1)} %copy-done, f32[256]{0:T(256)S(1)} %mul.162, f32[256,768]{1,0:T(8,128)} %fusion.26, bf16[256,2048]{1,0:T(8,128)(2,1)} %constant_dynamic-update-slice_fusion.5, bf16[1,2048,768]{2,1,0:T(8,128)(2,1)} %param.29), kind=kOutput, calls=%fused_computation.90 | convolution fusion | flops 1615986688 | bytes 10224640 | tf_op jit(solution)/shard_map/dot_general | solution.py:91
  177.8 5.9 %collective-permute-done.16 = bf16[128,2048]{1,0:T(8,128)(2,1)S(1)} collective-permute-done((bf16[128,2048]{1,0:T(8,128)(2,1)S(1)}, bf16[128,2048]{1,0:T(8,128)(2,1)S(1)}, u32[]{:S(2)}, u32[]{:S(2)}) %collective-permute-start.16) | collective-permute-done | bytes 524320 | tf_op jit(solution)/shard_map/ppermute | solution.py:84
  185.5 3.9 %collective-permute-done.27 = bf16[64,2048]{1,0:T(8,128)(2,1)S(1)} collective-permute-done((bf16[64,2048]{1,0:T(8,128)(2,1)S(1)}, bf16[64,2048]{1,0:T(8,128)(2,1)S(1)}, u32[]{:S(2)}, u32[]{:S(2)}) %collective-permute-start.27) | collective-permute-done | bytes 262176 | tf_op jit(solution)/shard_map/ppermute | solution.py:84
  195.9 3.3 %collective-permute-done.38 = bf16[32,2048]{1,0:T(8,128)(2,1)S(1)} collective-permute-done((bf16[32,2048]{1,0:T(8,128)(2,1)S(1)}, bf16[32,2048]{1,0:T(8,128)(2,1)S(1)}, u32[]{:S(2)}, u32[]{:S(2)}) %collective-permute-start.38) | collective-permute-done | bytes 131104 | tf_op jit(solution)/shard_map/ppermute | solution.py:84
  199.4 3.2 %collective-permute-done.8 = bf16[32,2048]{1,0:T(8,128)(2,1)S(1)} collective-permute-done((bf16[32,2048]{1,0:T(8,128)(2,1)S(1)}, bf16[32,2048]{1,0:T(8,128)(2,1)S(1)}, u32[]{:S(2)}, u32[]{:S(2)}) %collective-permute-start.8) | collective-permute-done | bytes 131104 | tf_op jit(solution)/shard_map/ppermute | solution.py:84
  202.7 1.7 collective-permute-done.18
  205.7 2.0 collective-permute-done.39
  208.6 1.8 collective-permute-done.19
  (227 shorter events, 84.0 us)
Async XLA Ops:
  10.9 21.7 %collective-permute-start.20 = (bf16[16,2048]{1,0:T(8,128)(2,1)}, bf16[16,2048]{1,0:T(8,128)(2,1)}, u32[]{:S(2)}, u32[]{:S(2)}) collective-permute-start(bf16[16,2048]{1,0:T(8,128)(2,1)} %get-tuple-element.20), channel_id=1, source_target_pairs={{0,16},{1,17},{2,18},{3,19},{4,20},{5,21},{6,22},{7,23},{8,24},{9,... | collective-permute-start | bytes 196616 | tf_op jit(solution)/shard_map/ppermute | solution.py:84
  16.0 12.6 %all-to-all-start = ((f32[2,32,32]{1,0,2:T(2,128)}), f32[2,32,32]{1,0,2:T(2,128)}, u32[]{:S(2)}, u32[]{:S(2)}) async-start(f32[2,32,32]{1,0,2:T(2,128)} %copy.30), calls=%async_computation | async-start | bytes 65536 | tf_op jit(solution)/shard_map/all_to_all | solution.py:120
  20.0 15.1 %collective-permute-start.30 = (bf16[16,2048]{1,0:T(8,128)(2,1)}, bf16[16,2048]{1,0:T(8,128)(2,1)}, u32[]{:S(2)}, u32[]{:S(2)}) collective-permute-start(bf16[16,2048]{1,0:T(8,128)(2,1)} %get-tuple-element.23), channel_id=1, source_target_pairs={{0,16},{1,17},{2,18},{3,19},{4,20},{5,21},{6,22},{7,23},{8,24},{9,... | collective-permute-start | bytes 196616 | tf_op jit(solution)/shard_map/ppermute | solution.py:84
  23.4 13.2 %collective-permute-start = (bf16[16,2048]{1,0:T(8,128)(2,1)}, bf16[16,2048]{1,0:T(8,128)(2,1)}, u32[]{:S(2)}, u32[]{:S(2)}) collective-permute-start(bf16[16,2048]{1,0:T(8,128)(2,1)} %get-tuple-element.16), channel_id=1, source_target_pairs={{0,16},{1,17},{2,18},{3,19},{4,20},{5,21},{6,22},{7,23},{8,24},{9,... | collective-permute-start | bytes 196616 | tf_op jit(solution)/shard_map/ppermute | solution.py:84
  23.7 15.3 %collective-permute-start.10 = (bf16[16,2048]{1,0:T(8,128)(2,1)}, bf16[16,2048]{1,0:T(8,128)(2,1)}, u32[]{:S(2)}, u32[]{:S(2)}) collective-permute-start(bf16[16,2048]{1,0:T(8,128)(2,1)} %get-tuple-element.19), channel_id=1, source_target_pairs={{0,16},{1,17},{2,18},{3,19},{4,20},{5,21},{6,22},{7,23},{8,24},{9,... | collective-permute-start | bytes 196616 | tf_op jit(solution)/shard_map/ppermute | solution.py:84
  33.5 12.9 %collective-permute-start.21 = (bf16[32,2048]{1,0:T(8,128)(2,1)S(1)}, bf16[32,2048]{1,0:T(8,128)(2,1)S(1)}, u32[]{:S(2)}, u32[]{:S(2)}) collective-permute-start(bf16[32,2048]{1,0:T(8,128)(2,1)S(1)} %pad_maximum_fusion.11), channel_id=1, source_target_pairs={{0,8},{1,9},{2,10},{3,11},{4,12},{5,13},{6,14},{7,15},{8,0},{9,1},... | collective-permute-start | bytes 393224 | tf_op jit(solution)/shard_map/ppermute | solution.py:84
  36.0 12.8 %collective-permute-start.31 = (bf16[32,2048]{1,0:T(8,128)(2,1)S(1)}, bf16[32,2048]{1,0:T(8,128)(2,1)S(1)}, u32[]{:S(2)}, u32[]{:S(2)}) collective-permute-start(bf16[32,2048]{1,0:T(8,128)(2,1)S(1)} %pad_maximum_fusion.12), channel_id=1, source_target_pairs={{0,8},{1,9},{2,10},{3,11},{4,12},{5,13},{6,14},{7,15},{8,0},{9,1},... | collective-permute-start | bytes 393224 | tf_op jit(solution)/shard_map/ppermute | solution.py:84
  37.4 13.8 %collective-permute-start.1 = (bf16[32,2048]{1,0:T(8,128)(2,1)S(1)}, bf16[32,2048]{1,0:T(8,128)(2,1)S(1)}, u32[]{:S(2)}, u32[]{:S(2)}) collective-permute-start(bf16[32,2048]{1,0:T(8,128)(2,1)S(1)} %pad_maximum_fusion.9), channel_id=1, source_target_pairs={{0,8},{1,9},{2,10},{3,11},{4,12},{5,13},{6,14},{7,15},{8,0},{9,1},... | collective-permute-start | bytes 393224 | tf_op jit(solution)/shard_map/ppermute | solution.py:84
  39.9 12.8 %collective-permute-start.11 = (bf16[32,2048]{1,0:T(8,128)(2,1)S(1)}, bf16[32,2048]{1,0:T(8,128)(2,1)S(1)}, u32[]{:S(2)}, u32[]{:S(2)}) collective-permute-start(bf16[32,2048]{1,0:T(8,128)(2,1)S(1)} %pad_maximum_fusion.10), channel_id=1, source_target_pairs={{0,8},{1,9},{2,10},{3,11},{4,12},{5,13},{6,14},{7,15},{8,0},{9,1},... | collective-permute-start | bytes 393224 | tf_op jit(solution)/shard_map/ppermute | solution.py:84
  52.2 9.7 %collective-permute-start.2 = (bf16[64,2048]{1,0:T(8,128)(2,1)S(1)}, bf16[64,2048]{1,0:T(8,128)(2,1)S(1)}, u32[]{:S(2)}, u32[]{:S(2)}) collective-permute-start(bf16[64,2048]{1,0:T(8,128)(2,1)S(1)} %pad_maximum_fusion.4), channel_id=1, source_target_pairs={{0,4},{1,5},{2,6},{3,7},{4,0},{5,1},{6,2},{7,3},{8,12},{9,13},{10,... | collective-permute-start | bytes 786440 | tf_op jit(solution)/shard_map/ppermute | solution.py:84
  53.6 10.6 %collective-permute-start.12 = (bf16[64,2048]{1,0:T(8,128)(2,1)S(1)}, bf16[64,2048]{1,0:T(8,128)(2,1)S(1)}, u32[]{:S(2)}, u32[]{:S(2)}) collective-permute-start(bf16[64,2048]{1,0:T(8,128)(2,1)S(1)} %pad_maximum_fusion.5), channel_id=1, source_target_pairs={{0,2},{1,3},{2,0},{3,1},{4,6},{5,7},{6,4},{7,5},{8,10},{9,11},{10,... | collective-permute-start | bytes 786440 | tf_op jit(solution)/shard_map/ppermute | solution.py:84
  57.8 17.7 %collective-permute-start.23 = (bf16[128,2048]{1,0:T(8,128)(2,1)S(1)}, bf16[128,2048]{1,0:T(8,128)(2,1)S(1)}, u32[]{:S(2)}, u32[]{:S(2)}) collective-permute-start(bf16[128,2048]{1,0:T(8,128)(2,1)S(1)} %pad_maximum_fusion.2), channel_id=1, source_target_pairs={{0,2},{1,3},{2,0},{3,1},{4,6},{5,7},{6,4},{7,5},{8,10},{9,11},{10,... | collective-permute-start | bytes 1572872 | tf_op jit(solution)/shard_map/ppermute | solution.py:84
  60.3 15.3 %collective-permute-start.33 = (bf16[128,2048]{1,0:T(8,128)(2,1)S(1)}, bf16[128,2048]{1,0:T(8,128)(2,1)S(1)}, u32[]{:S(2)}, u32[]{:S(2)}) collective-permute-start(bf16[128,2048]{1,0:T(8,128)(2,1)S(1)} %pad_maximum_fusion.3), channel_id=1, source_target_pairs={{0,4},{1,5},{2,6},{3,7},{4,0},{5,1},{6,2},{7,3},{8,12},{9,13},{10,... | collective-permute-start | bytes 1572872 | tf_op jit(solution)/shard_map/ppermute | solution.py:84
  62.8 21.4 %collective-permute-start.3 = (bf16[128,2048]{1,0:T(8,128)(2,1)S(1)}, bf16[128,2048]{1,0:T(8,128)(2,1)S(1)}, u32[]{:S(2)}, u32[]{:S(2)}) collective-permute-start(bf16[128,2048]{1,0:T(8,128)(2,1)S(1)} %pad_maximum_fusion), channel_id=1, source_target_pairs={{0,2},{1,3},{2,0},{3,1},{4,6},{5,7},{6,4},{7,5},{8,10},{9,11},{10,... | collective-permute-start | bytes 1572872 | tf_op jit(solution)/shard_map/ppermute | solution.py:84
  65.2 21.8 %collective-permute-start.13 = (bf16[128,2048]{1,0:T(8,128)(2,1)S(1)}, bf16[128,2048]{1,0:T(8,128)(2,1)S(1)}, u32[]{:S(2)}, u32[]{:S(2)}) collective-permute-start(bf16[128,2048]{1,0:T(8,128)(2,1)S(1)} %pad_maximum_fusion.1), channel_id=1, source_target_pairs={{0,4},{1,5},{2,6},{3,7},{4,0},{5,1},{6,2},{7,3},{8,12},{9,13},{10,... | collective-permute-start | bytes 1572872 | tf_op jit(solution)/shard_map/ppermute | solution.py:84
  75.5 22.0 %collective-permute-start.24 = (bf16[256,2048]{1,0:T(8,128)(2,1)S(1)}, bf16[256,2048]{1,0:T(8,128)(2,1)S(1)}, u32[]{:S(2)}, u32[]{:S(2)}) collective-permute-start(bf16[256,2048]{1,0:T(8,128)(2,1)S(1)} %constant_dynamic-update-slice_fusion.10), channel_id=1, source_target_pairs={{0,1},{1,0},{2,3},{3,2},{4,5},{5,4},{6,7},{7,6},{8,9},{9,8},{10,11... | collective-permute-start | bytes 3145736 | tf_op jit(solution)/shard_map/ppermute | solution.py:84
  76.7 29.3 %collective-permute-start.34 = (bf16[256,2048]{1,0:T(8,128)(2,1)}, bf16[256,2048]{1,0:T(8,128)(2,1)}, u32[]{:S(2)}, u32[]{:S(2)}) collective-permute-start(bf16[256,2048]{1,0:T(8,128)(2,1)} %constant_dynamic-update-slice_fusion.15), channel_id=1, source_target_pairs={{0,1},{1,0},{2,3},{3,2},{4,5},{5,4},{6,7},{7,6},{8,9},{9,8},{10,11... | collective-permute-start | bytes 3145736 | tf_op jit(solution)/shard_map/ppermute | solution.py:84
  85.1 31.0 %collective-permute-start.4 = (bf16[256,2048]{1,0:T(8,128)(2,1)}, bf16[256,2048]{1,0:T(8,128)(2,1)}, u32[]{:S(2)}, u32[]{:S(2)}) collective-permute-start(bf16[256,2048]{1,0:T(8,128)(2,1)} %constant_dynamic-update-slice_fusion), channel_id=1, source_target_pairs={{0,1},{1,0},{2,3},{3,2},{4,5},{5,4},{6,7},{7,6},{8,9},{9,8},{10,11... | collective-permute-start | bytes 3145736 | tf_op jit(solution)/shard_map/ppermute | solution.py:84
  87.8 38.1 %collective-permute-start.14 = (bf16[256,2048]{1,0:T(8,128)(2,1)}, bf16[256,2048]{1,0:T(8,128)(2,1)}, u32[]{:S(2)}, u32[]{:S(2)}) collective-permute-start(bf16[256,2048]{1,0:T(8,128)(2,1)} %constant_dynamic-update-slice_fusion.5), channel_id=1, source_target_pairs={{0,1},{1,0},{2,3},{3,2},{4,5},{5,4},{6,7},{7,6},{8,9},{9,8},{10,11... | collective-permute-start | bytes 3145736 | tf_op jit(solution)/shard_map/ppermute | solution.py:84
  106.0 30.0 %collective-permute-start.25 = (bf16[256,2048]{1,0:T(8,128)(2,1)}, bf16[256,2048]{1,0:T(8,128)(2,1)}, u32[]{:S(2)}, u32[]{:S(2)}) collective-permute-start(bf16[256,2048]{1,0:T(8,128)(2,1)} %fusion.126), channel_id=1, source_target_pairs={{0,1},{1,0},{2,3},{3,2},{4,5},{5,4},{6,7},{7,6},{8,9},{9,8},{10,11... | collective-permute-start | bytes 3145736 | tf_op jit(solution)/shard_map/ppermute | solution.py:84
  115.6 29.4 %collective-permute-start.35 = (bf16[256,2048]{1,0:T(8,128)(2,1)}, bf16[256,2048]{1,0:T(8,128)(2,1)}, u32[]{:S(2)}, u32[]{:S(2)}) collective-permute-start(bf16[256,2048]{1,0:T(8,128)(2,1)} %fusion.153), channel_id=1, source_target_pairs={{0,1},{1,0},{2,3},{3,2},{4,5},{5,4},{6,7},{7,6},{8,9},{9,8},{10,11... | collective-permute-start | bytes 3145736 | tf_op jit(solution)/shard_map/ppermute | solution.py:84
  125.8 27.6 %collective-permute-start.5 = (bf16[256,2048]{1,0:T(8,128)(2,1)}, bf16[256,2048]{1,0:T(8,128)(2,1)}, u32[]{:S(2)}, u32[]{:S(2)}) collective-permute-start(bf16[256,2048]{1,0:T(8,128)(2,1)} %fusion.72), channel_id=1, source_target_pairs={{0,1},{1,0},{2,3},{3,2},{4,5},{5,4},{6,7},{7,6},{8,9},{9,8},{10,11... | collective-permute-start | bytes 3145736 | tf_op jit(solution)/shard_map/ppermute | solution.py:84
  135.4 26.3 %collective-permute-start.15 = (bf16[256,2048]{1,0:T(8,128)(2,1)}, bf16[256,2048]{1,0:T(8,128)(2,1)}, u32[]{:S(2)}, u32[]{:S(2)}) collective-permute-start(bf16[256,2048]{1,0:T(8,128)(2,1)} %fusion.99), channel_id=1, source_target_pairs={{0,1},{1,0},{2,3},{3,2},{4,5},{5,4},{6,7},{7,6},{8,9},{9,8},{10,11... | collective-permute-start | bytes 3145736 | tf_op jit(solution)/shard_map/ppermute | solution.py:84
  143.7 26.7 %collective-permute-start.26 = (bf16[128,2048]{1,0:T(8,128)(2,1)}, bf16[128,2048]{1,0:T(8,128)(2,1)}, u32[]{:S(2)}, u32[]{:S(2)}) collective-permute-start(bf16[128,2048]{1,0:T(8,128)(2,1)} %slice.255), channel_id=1, source_target_pairs={{0,2},{1,3},{2,0},{3,1},{4,6},{5,7},{6,4},{7,5},{8,10},{9,11},{10,... | collective-permute-start | bytes 1572872 | tf_op jit(solution)/shard_map/ppermute | solution.py:84
  152.7 19.9 %collective-permute-start.36 = (bf16[128,2048]{1,0:T(8,128)(2,1)}, bf16[128,2048]{1,0:T(8,128)(2,1)}, u32[]{:S(2)}, u32[]{:S(2)}) collective-permute-start(bf16[128,2048]{1,0:T(8,128)(2,1)} %slice.267), channel_id=1, source_target_pairs={{0,4},{1,5},{2,6},{3,7},{4,0},{5,1},{6,2},{7,3},{8,12},{9,13},{10,... | collective-permute-start | bytes 1572872 | tf_op jit(solution)/shard_map/ppermute | solution.py:84
  161.2 14.1 %collective-permute-start.6 = (bf16[128,2048]{1,0:T(8,128)(2,1)}, bf16[128,2048]{1,0:T(8,128)(2,1)}, u32[]{:S(2)}, u32[]{:S(2)}) collective-permute-start(bf16[128,2048]{1,0:T(8,128)(2,1)} %slice.231), channel_id=1, source_target_pairs={{0,2},{1,3},{2,0},{3,1},{4,6},{5,7},{6,4},{7,5},{8,10},{9,11},{10,... | collective-permute-start | bytes 1572872 | tf_op jit(solution)/shard_map/ppermute | solution.py:84
  168.9 14.9 %collective-permute-start.16 = (bf16[128,2048]{1,0:T(8,128)(2,1)S(1)}, bf16[128,2048]{1,0:T(8,128)(2,1)S(1)}, u32[]{:S(2)}, u32[]{:S(2)}) collective-permute-start(bf16[128,2048]{1,0:T(8,128)(2,1)S(1)} %slice.243), channel_id=1, source_target_pairs={{0,4},{1,5},{2,6},{3,7},{4,0},{5,1},{6,2},{7,3},{8,12},{9,13},{10,... | collective-permute-start | bytes 1572872 | tf_op jit(solution)/shard_map/ppermute | solution.py:84
  172.0 17.4 %collective-permute-start.27 = (bf16[64,2048]{1,0:T(8,128)(2,1)S(1)}, bf16[64,2048]{1,0:T(8,128)(2,1)S(1)}, u32[]{:S(2)}, u32[]{:S(2)}) collective-permute-start(bf16[64,2048]{1,0:T(8,128)(2,1)S(1)} %slice.257), channel_id=1, source_target_pairs={{0,4},{1,5},{2,6},{3,7},{4,0},{5,1},{6,2},{7,3},{8,12},{9,13},{10,... | collective-permute-start | bytes 786440 | tf_op jit(solution)/shard_map/ppermute | solution.py:84
  173.8 17.3 %collective-permute-start.37 = (bf16[64,2048]{1,0:T(8,128)(2,1)S(1)}, bf16[64,2048]{1,0:T(8,128)(2,1)S(1)}, u32[]{:S(2)}, u32[]{:S(2)}) collective-permute-start(bf16[64,2048]{1,0:T(8,128)(2,1)S(1)} %slice.269), channel_id=1, source_target_pairs={{0,2},{1,3},{2,0},{3,1},{4,6},{5,7},{6,4},{7,5},{8,10},{9,11},{10,... | collective-permute-start | bytes 786440 | tf_op jit(solution)/shard_map/ppermute | solution.py:84
  176.5 16.6 %collective-permute-start.7 = (bf16[64,2048]{1,0:T(8,128)(2,1)S(1)}, bf16[64,2048]{1,0:T(8,128)(2,1)S(1)}, u32[]{:S(2)}, u32[]{:S(2)}) collective-permute-start(bf16[64,2048]{1,0:T(8,128)(2,1)S(1)} %slice.233), channel_id=1, source_target_pairs={{0,4},{1,5},{2,6},{3,7},{4,0},{5,1},{6,2},{7,3},{8,12},{9,13},{10,... | collective-permute-start | bytes 786440 | tf_op jit(solution)/shard_map/ppermute | solution.py:84
  184.0 10.9 %collective-permute-start.17 = (bf16[64,2048]{1,0:T(8,128)(2,1)S(1)}, bf16[64,2048]{1,0:T(8,128)(2,1)S(1)}, u32[]{:S(2)}, u32[]{:S(2)}) collective-permute-start(bf16[64,2048]{1,0:T(8,128)(2,1)S(1)} %slice.245), channel_id=1, source_target_pairs={{0,2},{1,3},{2,0},{3,1},{4,6},{5,7},{6,4},{7,5},{8,10},{9,11},{10,... | collective-permute-start | bytes 786440 | tf_op jit(solution)/shard_map/ppermute | solution.py:84
  195.6 10.1 %collective-permute-start.29 = (bf16[16,2048]{1,0:T(8,128)(2,1)S(1)}, bf16[16,2048]{1,0:T(8,128)(2,1)S(1)}, u32[]{:S(2)}, u32[]{:S(2)}) collective-permute-start(bf16[16,2048]{1,0:T(8,128)(2,1)S(1)} %slice.261), channel_id=1, source_target_pairs={{0,16},{1,17},{2,18},{3,19},{4,20},{5,21},{6,22},{7,23},{8,24},{9,... | collective-permute-start | bytes 196616 | tf_op jit(solution)/shard_map/ppermute | solution.py:84
  (37 other events, 425.8 us)

commit v3 on v2

--- a/solution.py
+++ b/solution.py
@@ -84,13 +84,60 @@
     return lax.ppermute(x, "ex", [(i, i ^ (1 << bit)) for i in range(shards)])
 
 
-def weighted_rows(flat, weight, gate_proj, up_proj, down_proj):
-    gate = jnp.dot(flat, gate_proj[0], preferred_element_type=jnp.float32)
-    upper = jnp.dot(flat, up_proj[0], preferred_element_type=jnp.float32)
-    hidden = (jax.nn.silu(gate) * upper).astype(jnp.bfloat16)
-    out = jnp.dot(hidden, down_proj[0], preferred_element_type=jnp.float32)
-    out = out.astype(jnp.bfloat16).astype(jnp.float32)
-    return (weight * out).astype(jnp.bfloat16)
+def expert_kernel(
+    near_ref, far_ref, near_w, far_w, gate_ref, up_ref, down_ref, near_out, far_out, total
+):
+    step = pl.program_id(0)
+    last = pl.num_programs(0) - 1
+    for side, x_ref, w_ref, out_ref in ((0, near_ref, near_w, near_out), (1, far_ref, far_w, far_out)):
+        x = x_ref[...]
+        gate = jnp.dot(x, gate_ref[0], preferred_element_type=jnp.float32)
+        upper = jnp.dot(x, up_ref[0], preferred_element_type=jnp.float32)
+        hidden = (jax.nn.silu(gate) * upper).astype(jnp.bfloat16)
+        part = jnp.dot(hidden, down_ref[0], preferred_element_type=jnp.float32)
+
+        @pl.when(step == 0)
+        def _():
+            total[side] = part
+
+        @pl.when(step > 0)
+        def _():
+            total[side] += part
+
+        @pl.when(step == last)
+        def _():
+            out = total[side].astype(jnp.bfloat16).astype(jnp.float32)
+            out_ref[...] = (w_ref[...] * out).astype(jnp.bfloat16)
+
+
+def weighted_rows(near, far, near_w, far_w, gate_proj, up_proj, down_proj):
+    rows, width = near.shape
+    hidden = gate_proj.shape[2]
+    tile = 256 if hidden % 256 == 0 else hidden
+    whole = pl.BlockSpec((rows, width), lambda f: (0, 0))
+    column = pl.BlockSpec((rows, 1), lambda f: (0, 0))
+    return pl.pallas_call(
+        expert_kernel,
+        out_shape=[jax.ShapeDtypeStruct((rows, width), jnp.bfloat16)] * 2,
+        grid=(hidden // tile,),
+        in_specs=[
+            whole,
+            whole,
+            column,
+            column,
+            pl.BlockSpec((1, width, tile), lambda f: (0, 0, f)),
+            pl.BlockSpec((1, width, tile), lambda f: (0, 0, f)),
+            pl.BlockSpec((1, tile, width), lambda f: (0, f, 0)),
+        ],
+        out_specs=[whole, whole],
+        scratch_shapes=[pltpu.VMEM((2, rows, width), jnp.float32)],
+        compiler_params=pltpu.CompilerParams(vmem_limit_bytes=52 << 20),
+        cost_estimate=pl.CostEstimate(
+            flops=12 * rows * width * hidden,
+            bytes_accessed=6 * width * hidden + 8 * rows * width,
+            transcendentals=2 * rows * hidden,
+        ),
+    )(near, far, near_w, far_w, gate_proj, up_proj, down_proj)
 
 
 def wide_sum(a, b):
@@ -151,10 +198,10 @@
         for bit in order[:-1]:
             buf = jnp.concatenate([buf, swap(buf, bit, shards)], axis=0)
         far = swap(buf, order[-1], shards)
-        back = swap(
-            weighted_rows(far, weight[1], gate_proj, up_proj, down_proj), order[-1], shards
+        near_out, far_out = weighted_rows(
+            buf, far, weight[0], weight[1], gate_proj, up_proj, down_proj
         )
-        acc = wide_sum(weighted_rows(buf, weight[0], gate_proj, up_proj, down_proj), back)
+        acc = wide_sum(near_out, swap(far_out, order[-1], shards))
         for bit in order[-2::-1]:
             keep = acc.shape[0] // 2
             acc = wide_sum(acc[:keep], swap(acc[keep:], bit, shards))

time: 213 us -> 182 us (0.85)
  matrix products: 70.9 us -> 0 us
  Pallas kernels: 2.19 us -> 49.5 us
  waiting for transfers between devices: 39.9 us -> 65 us
  local copies, waits for them, and re-layouts: 37.3 us -> 17.5 us
  other arithmetic: 16.9 us -> 3.89 us
    dot_general x16 -> x0, matrix products: 70.9 us -> none  [the longest x8 45.5 us: weighted_rows(): out = jnp.dot(hidden, down_proj[0], preferred_element_type=jnp.float32)]
    pallas_call x0 -> x4, Pallas kernels: none -> 47.3 us  [weighted_rows(): pl.pallas_call(expert_kernel, out_shape=[jax.ShapeDtypeStruct((rows, widt...]
    ppermute x40, waiting for transfers between devices: 39.9 us -> 64.2 us  [swap(): return lax.ppermute(x, 'ex', [(i, i ^ 1 << bit) for i in range(shards)])]
    concatenate x12, other arithmetic: 10.7 us -> 0.28 us  [on_device(): buf = jnp.concatenate([buf, swap(buf, bit, shards)], axis=0)]
    unnamed x70 -> x60, local copies, waits for them, and re-layouts: 19.1 us -> 10.9 us
    slice x16, local copies, waits for them, and re-layouts: 6.99 us -> 0.3 us  [on_device(): acc = wide_sum(acc[:keep], swap(acc[keep:], bit, shards))]
    concatenate x4, local copies, waits for them, and re-layouts: 2.79 us -> 0.17 us  [on_device(): buf = jnp.concatenate([buf, swap(buf, bit, shards)], axis=0)]
    convert_element_type x12 -> x16, other arithmetic: 4.4 us -> 2.45 us  [wide_sum(): return (a.astype(jnp.float32) + b.astype(jnp.float32)).astype(jnp.bfloat16)]
  transfers between devices with their start and end apart: 41 -> 41, of which waited for: 12 -> 19; matrix products, arithmetic and copies ran while one was open for 54% -> 6% of each run, Pallas kernels for 0% -> 26%
where the time goes in v3:
time: 182 us
  waiting for transfers between devices  65 us (36%)
  Pallas kernels  49.5 us (27%)
  starting transfers between devices  45.1 us (25%)
  local copies, waits for them, and re-layouts  17.5 us (10%)
  other arithmetic  3.89 us (2%)
    ppermute x40, waiting for transfers between devices, swap(): return lax.ppermute(x, 'ex', [(i, i ^ 1 << bit) for i in range(shards)])  64.2 us
    pallas_call x4, Pallas kernels, weighted_rows(): pl.pallas_call(expert_kernel, out_shape=[jax.ShapeDtypeStruct((rows, widt...  47.3 us
    ppermute x40, starting transfers between devices, swap(): return lax.ppermute(x, 'ex', [(i, i ^ 1 << bit) for i in range(shards)])  41.3 us
    unnamed x60, local copies, waits for them, and re-layouts  10.9 us
    all_to_all x1, starting transfers between devices, on_device(): mine = lax.all_to_all(table, 'ex', split_axis=2, concat_axis=1, tiled=True)  3.82 us
  transfers between devices with their start and end apart: 41, of which 19 were waited for; matrix products, arithmetic and copies ran while one was open for 6% of the time, Pallas kernels for 26%

profile of v3, /device:TPU:0, one launch (start us, length us, event | category | flops | bytes accessed | tf_op | source)
XLA Modules:
  0.0 181.9 jit_solution(2334616278720894188)
XLA Ops:
  1.8 1.6 copy-done
  3.4 1.6 copy-done.1
  9.3 4.0 %collective-permute-start.20 = (bf16[16,2048]{1,0:T(8,128)(2,1)S(1)}, bf16[16,2048]{1,0:T(8,128)(2,1)S(1)}, u32[]{:S(2)}, u32[]{:S(2)}) collective-permute-start(bf16[16,2048]{1,0:T(8,128)(2,1)S(1)} %get-tuple-element.36), channel_id=1, source_target_pairs={{0,16},{1,17},{2,18},{3,19},{4,20},{5,21},{6,22},{7,23},{8,24},{9,... | collective-permute-start | bytes 196616 | tf_op jit(solution)/shard_map/ppermute | solution.py:84
  14.5 3.8 %all-to-all-start = ((f32[2,32,32]{1,0,2:T(2,128)}), f32[2,32,32]{1,0,2:T(2,128)S(1)}, u32[]{:S(2)}, u32[]{:S(2)}) async-start(f32[2,32,32]{1,0,2:T(2,128)} %copy.50), calls=%async_computation | async-start | bytes 65536 | tf_op jit(solution)/shard_map/all_to_all | solution.py:167
  18.3 2.7 %collective-permute-start.30 = (bf16[16,2048]{1,0:T(8,128)(2,1)S(1)}, bf16[16,2048]{1,0:T(8,128)(2,1)S(1)}, u32[]{:S(2)}, u32[]{:S(2)}) collective-permute-start(bf16[16,2048]{1,0:T(8,128)(2,1)S(1)} %get-tuple-element.39), channel_id=1, source_target_pairs={{0,16},{1,17},{2,18},{3,19},{4,20},{5,21},{6,22},{7,23},{8,24},{9,... | collective-permute-start | bytes 196616 | tf_op jit(solution)/shard_map/ppermute | solution.py:84
  22.0 2.7 %collective-permute-start.10 = (bf16[16,2048]{1,0:T(8,128)(2,1)S(1)}, bf16[16,2048]{1,0:T(8,128)(2,1)S(1)}, u32[]{:S(2)}, u32[]{:S(2)}) collective-permute-start(bf16[16,2048]{1,0:T(8,128)(2,1)S(1)} %get-tuple-element.35), channel_id=1, source_target_pairs={{0,16},{1,17},{2,18},{3,19},{4,20},{5,21},{6,22},{7,23},{8,24},{9,... | collective-permute-start | bytes 196616 | tf_op jit(solution)/shard_map/ppermute | solution.py:84
  29.9 1.4 collective-permute-start.31
  32.1 1.4 collective-permute-start.11
  36.3 2.0 %collective-permute-done.31 = bf16[32,2048]{1,0:T(8,128)(2,1)S(1)} collective-permute-done((bf16[32,2048]{1,0:T(8,128)(2,1)S(1)}, bf16[32,2048]{1,0:T(8,128)(2,1)S(1)}, u32[]{:S(2)}, u32[]{:S(2)}) %collective-permute-start.31) | collective-permute-done | bytes 131104 | tf_op jit(solution)/shard_map/ppermute | solution.py:84
  39.1 2.0 %collective-permute-done.1 = bf16[32,2048]{1,0:T(8,128)(2,1)S(1)} collective-permute-done((bf16[32,2048]{1,0:T(8,128)(2,1)S(1)}, bf16[32,2048]{1,0:T(8,128)(2,1)S(1)}, u32[]{:S(2)}, u32[]{:S(2)}) %collective-permute-start.1) | collective-permute-done | bytes 131104 | tf_op jit(solution)/shard_map/ppermute | solution.py:84
  41.9 1.2 collective-permute-done.11
  44.2 1.2 collective-permute-start.23
  46.4 3.2 %collective-permute-done.2 = bf16[64,2048]{1,0:T(8,128)(2,1)S(1)} collective-permute-done((bf16[64,2048]{1,0:T(8,128)(2,1)S(1)}, bf16[64,2048]{1,0:T(8,128)(2,1)S(1)}, u32[]{:S(2)}, u32[]{:S(2)}) %collective-permute-start.2) | collective-permute-done | bytes 262176 | tf_op jit(solution)/shard_map/ppermute | solution.py:84
  49.9 2.5 %collective-permute-done.12 = bf16[64,2048]{1,0:T(8,128)(2,1)S(1)} collective-permute-done((bf16[64,2048]{1,0:T(8,128)(2,1)S(1)}, bf16[64,2048]{1,0:T(8,128)(2,1)S(1)}, u32[]{:S(2)}, u32[]{:S(2)}) %collective-permute-start.12) | collective-permute-done | bytes 262176 | tf_op jit(solution)/shard_map/ppermute | solution.py:84
  53.5 10.2 %collective-permute-done.23 = bf16[128,2048]{1,0:T(8,128)(2,1)S(1)} collective-permute-done((bf16[128,2048]{1,0:T(8,128)(2,1)S(1)}, bf16[128,2048]{1,0:T(8,128)(2,1)S(1)}, u32[]{:S(2)}, u32[]{:S(2)}) %collective-permute-start.23) | collective-permute-done | bytes 524320 | tf_op jit(solution)/shard_map/ppermute | solution.py:84
  64.4 8.7 %collective-permute-done.3 = bf16[128,2048]{1,0:T(8,128)(2,1)S(1)} collective-permute-done((bf16[128,2048]{1,0:T(8,128)(2,1)S(1)}, bf16[128,2048]{1,0:T(8,128)(2,1)S(1)}, u32[]{:S(2)}, u32[]{:S(2)}) %collective-permute-start.3) | collective-permute-done | bytes 524320 | tf_op jit(solution)/shard_map/ppermute | solution.py:84
  74.9 11.8 %shard_map.167 = (bf16[256,2048]{1,0:T(8,128)(2,1)S(1)}, bf16[256,2048]{1,0:T(8,128)(2,1)}) custom-call(bf16[256,2048]{1,0:T(8,128)(2,1)} %copy-done.10, bf16[256,2048]{1,0:T(8,128)(2,1)} %copy-done.19, f32[256,1]{1,0:T(8,128)S(1)} %squeeze.56.near_w, f32[256,1]{1,0:T(8,128)S(1)} %squeeze.57.far_w, bf16[1,2048,768]{2,1,0:T(8,128)(2,1)} %gate_ref.7, ...), custom_call_target="tpu_custom_call" | custom-call | flops 4831838208 | bytes 13631488 | tf_op jit(solution)/shard_map/pallas_call | solution.py:119
  87.9 11.9 %shard_map.168 = (bf16[256,2048]{1,0:T(8,128)(2,1)S(1)}, bf16[256,2048]{1,0:T(8,128)(2,1)}) custom-call(bf16[256,2048]{1,0:T(8,128)(2,1)} %copy-done.8, bf16[256,2048]{1,0:T(8,128)(2,1)} %copy-done.20, f32[256,1]{1,0:T(8,128)S(1)} %squeeze.58.near_w, f32[256,1]{1,0:T(8,128)S(1)} %squeeze.59.far_w, bf16[1,2048,768]{2,1,0:T(8,128)(2,1)} %gate_ref.7, ...), custom_call_target="tpu_custom_call" | custom-call | flops 4831838208 | bytes 13631488 | tf_op jit(solution)/shard_map/pallas_call | solution.py:119
  100.2 11.8 %shard_map.164 = (bf16[256,2048]{1,0:T(8,128)(2,1)S(1)}, bf16[256,2048]{1,0:T(8,128)(2,1)}) custom-call(bf16[256,2048]{1,0:T(8,128)(2,1)} %copy-done.14, bf16[256,2048]{1,0:T(8,128)(2,1)} %collective-permute-done.4.far_ref, f32[256,1]{1,0:T(8,128)S(1)} %squeeze.52.near_w, f32[256,1]{1,0:T(8,128)S(1)} %squeeze.53.far_w, bf16[1,2048,768]{2,1,0:T(8,128)(2,1)} %gate_ref.7, ...), custom_call_target="tpu_custom_call" | custom-call | flops 4831838208 | bytes 13631488 | tf_op jit(solution)/shard_map/pallas_call | solution.py:119
  113.1 11.8 %shard_map.165 = (bf16[256,2048]{1,0:T(8,128)(2,1)S(1)}, bf16[256,2048]{1,0:T(8,128)(2,1)}) custom-call(bf16[256,2048]{1,0:T(8,128)(2,1)} %copy-done.12, bf16[256,2048]{1,0:T(8,128)(2,1)} %copy-done.18, f32[256,1]{1,0:T(8,128)S(1)} %squeeze.54.near_w, f32[256,1]{1,0:T(8,128)S(1)} %squeeze.55.far_w, bf16[1,2048,768]{2,1,0:T(8,128)(2,1)} %gate_ref.7, ...), custom_call_target="tpu_custom_call" | custom-call | flops 4831838208 | bytes 13631488 | tf_op jit(solution)/shard_map/pallas_call | solution.py:119
  127.3 1.5 collective-permute-start.36
  131.4 9.2 %collective-permute-done.26 = bf16[128,2048]{1,0:T(8,128)(2,1)S(1)} collective-permute-done((bf16[128,2048]{1,0:T(8,128)(2,1)S(1)}, bf16[128,2048]{1,0:T(8,128)(2,1)S(1)}, u32[]{:S(2)}, u32[]{:S(2)}) %collective-permute-start.26) | collective-permute-done | bytes 524320 | tf_op jit(solution)/shard_map/ppermute | solution.py:84
  143.5 8.3 %collective-permute-done.6 = bf16[128,2048]{1,0:T(8,128)(2,1)S(1)} collective-permute-done((bf16[128,2048]{1,0:T(8,128)(2,1)S(1)}, bf16[128,2048]{1,0:T(8,128)(2,1)S(1)}, u32[]{:S(2)}, u32[]{:S(2)}) %collective-permute-start.6) | collective-permute-done | bytes 524320 | tf_op jit(solution)/shard_map/ppermute | solution.py:84
  154.7 4.3 %collective-permute-done.27 = bf16[64,2048]{1,0:T(8,128)(2,1)S(1)} collective-permute-done((bf16[64,2048]{1,0:T(8,128)(2,1)S(1)}, bf16[64,2048]{1,0:T(8,128)(2,1)S(1)}, u32[]{:S(2)}, u32[]{:S(2)}) %collective-permute-start.27) | collective-permute-done | bytes 262176 | tf_op jit(solution)/shard_map/ppermute | solution.py:84
  161.4 2.1 %collective-permute-done.7 = bf16[64,2048]{1,0:T(8,128)(2,1)S(1)} collective-permute-done((bf16[64,2048]{1,0:T(8,128)(2,1)S(1)}, bf16[64,2048]{1,0:T(8,128)(2,1)S(1)}, u32[]{:S(2)}, u32[]{:S(2)}) %collective-permute-start.7) | collective-permute-done | bytes 262176 | tf_op jit(solution)/shard_map/ppermute | solution.py:84
  165.9 1.9 %collective-permute-start.29 = (bf16[16,2048]{1,0:T(8,128)(2,1)S(1)}, bf16[16,2048]{1,0:T(8,128)(2,1)S(1)}, u32[]{:S(2)}, u32[]{:S(2)}) collective-permute-start(bf16[16,2048]{1,0:T(8,128)(2,1)S(1)} %slice.261), channel_id=1, source_target_pairs={{0,16},{1,17},{2,18},{3,19},{4,20},{5,21},{6,22},{7,23},{8,24},{9,... | collective-permute-start | bytes 196616 | tf_op jit(solution)/shard_map/ppermute | solution.py:84
  167.9 1.4 collective-permute-start.39
  169.3 3.5 %collective-permute-done.8 = bf16[32,2048]{1,0:T(8,128)(2,1)S(1)} collective-permute-done((bf16[32,2048]{1,0:T(8,128)(2,1)S(1)}, bf16[32,2048]{1,0:T(8,128)(2,1)S(1)}, u32[]{:S(2)}, u32[]{:S(2)}) %collective-permute-start.8) | collective-permute-done | bytes 131104 | tf_op jit(solution)/shard_map/ppermute | solution.py:84
  173.3 1.4 collective-permute-done.18
  174.8 1.2 collective-permute-start.19
  176.0 3.6 %collective-permute-done.9 = bf16[16,2048]{1,0:T(8,128)(2,1)S(1)} collective-permute-done((bf16[16,2048]{1,0:T(8,128)(2,1)S(1)}, bf16[16,2048]{1,0:T(8,128)(2,1)S(1)}, u32[]{:S(2)}, u32[]{:S(2)}) %collective-permute-start.9) | collective-permute-done | bytes 65568 | tf_op jit(solution)/shard_map/ppermute | solution.py:84
  179.6 1.4 collective-permute-done.19
  (209 shorter events, 44.0 us)
Async XLA Ops:
  9.3 19.7 %collective-permute-start.20 = (bf16[16,2048]{1,0:T(8,128)(2,1)S(1)}, bf16[16,2048]{1,0:T(8,128)(2,1)S(1)}, u32[]{:S(2)}, u32[]{:S(2)}) collective-permute-start(bf16[16,2048]{1,0:T(8,128)(2,1)S(1)} %get-tuple-element.36), channel_id=1, source_target_pairs={{0,16},{1,17},{2,18},{3,19},{4,20},{5,21},{6,22},{7,23},{8,24},{9,... | collective-permute-start | bytes 196616 | tf_op jit(solution)/shard_map/ppermute | solution.py:84
  14.5 11.2 %all-to-all-start = ((f32[2,32,32]{1,0,2:T(2,128)}), f32[2,32,32]{1,0,2:T(2,128)S(1)}, u32[]{:S(2)}, u32[]{:S(2)}) async-start(f32[2,32,32]{1,0,2:T(2,128)} %copy.50), calls=%async_computation | async-start | bytes 65536 | tf_op jit(solution)/shard_map/all_to_all | solution.py:167
  18.3 11.6 %collective-permute-start.30 = (bf16[16,2048]{1,0:T(8,128)(2,1)S(1)}, bf16[16,2048]{1,0:T(8,128)(2,1)S(1)}, u32[]{:S(2)}, u32[]{:S(2)}) collective-permute-start(bf16[16,2048]{1,0:T(8,128)(2,1)S(1)} %get-tuple-element.39), channel_id=1, source_target_pairs={{0,16},{1,17},{2,18},{3,19},{4,20},{5,21},{6,22},{7,23},{8,24},{9,... | collective-permute-start | bytes 196616 | tf_op jit(solution)/shard_map/ppermute | solution.py:84
  21.7 9.5 %collective-permute-start = (bf16[16,2048]{1,0:T(8,128)(2,1)S(1)}, bf16[16,2048]{1,0:T(8,128)(2,1)S(1)}, u32[]{:S(2)}, u32[]{:S(2)}) collective-permute-start(bf16[16,2048]{1,0:T(8,128)(2,1)S(1)} %get-tuple-element.32), channel_id=1, source_target_pairs={{0,16},{1,17},{2,18},{3,19},{4,20},{5,21},{6,22},{7,23},{8,24},{9,... | collective-permute-start | bytes 196616 | tf_op jit(solution)/shard_map/ppermute | solution.py:84
  22.0 10.1 %collective-permute-start.10 = (bf16[16,2048]{1,0:T(8,128)(2,1)S(1)}, bf16[16,2048]{1,0:T(8,128)(2,1)S(1)}, u32[]{:S(2)}, u32[]{:S(2)}) collective-permute-start(bf16[16,2048]{1,0:T(8,128)(2,1)S(1)} %get-tuple-element.35), channel_id=1, source_target_pairs={{0,16},{1,17},{2,18},{3,19},{4,20},{5,21},{6,22},{7,23},{8,24},{9,... | collective-permute-start | bytes 196616 | tf_op jit(solution)/shard_map/ppermute | solution.py:84
  31.2 9.8 %collective-permute-start.1 = (bf16[32,2048]{1,0:T(8,128)(2,1)S(1)}, bf16[32,2048]{1,0:T(8,128)(2,1)S(1)}, u32[]{:S(2)}, u32[]{:S(2)}) collective-permute-start(bf16[32,2048]{1,0:T(8,128)(2,1)S(1)} %pad_maximum_fusion.9), channel_id=1, source_target_pairs={{0,8},{1,9},{2,10},{3,11},{4,12},{5,13},{6,14},{7,15},{8,0},{9,1},... | collective-permute-start | bytes 393224 | tf_op jit(solution)/shard_map/ppermute | solution.py:84
  32.1 11.0 %collective-permute-start.11 = (bf16[32,2048]{1,0:T(8,128)(2,1)S(1)}, bf16[32,2048]{1,0:T(8,128)(2,1)S(1)}, u32[]{:S(2)}, u32[]{:S(2)}) collective-permute-start(bf16[32,2048]{1,0:T(8,128)(2,1)S(1)} %pad_maximum_fusion.10), channel_id=1, source_target_pairs={{0,8},{1,9},{2,10},{3,11},{4,12},{5,13},{6,14},{7,15},{8,0},{9,1},... | collective-permute-start | bytes 393224 | tf_op jit(solution)/shard_map/ppermute | solution.py:84
  35.5 8.6 %collective-permute-start.22 = (bf16[64,2048]{1,0:T(8,128)(2,1)S(1)}, bf16[64,2048]{1,0:T(8,128)(2,1)S(1)}, u32[]{:S(2)}, u32[]{:S(2)}) collective-permute-start(bf16[64,2048]{1,0:T(8,128)(2,1)S(1)} %pad_maximum_fusion.6), channel_id=1, source_target_pairs={{0,4},{1,5},{2,6},{3,7},{4,0},{5,1},{6,2},{7,3},{8,12},{9,13},{10,... | collective-permute-start | bytes 786440 | tf_op jit(solution)/shard_map/ppermute | solution.py:84
  41.1 8.5 %collective-permute-start.2 = (bf16[64,2048]{1,0:T(8,128)(2,1)S(1)}, bf16[64,2048]{1,0:T(8,128)(2,1)S(1)}, u32[]{:S(2)}, u32[]{:S(2)}) collective-permute-start(bf16[64,2048]{1,0:T(8,128)(2,1)S(1)} %pad_maximum_fusion.4), channel_id=1, source_target_pairs={{0,4},{1,5},{2,6},{3,7},{4,0},{5,1},{6,2},{7,3},{8,12},{9,13},{10,... | collective-permute-start | bytes 786440 | tf_op jit(solution)/shard_map/ppermute | solution.py:84
  43.1 9.3 %collective-permute-start.12 = (bf16[64,2048]{1,0:T(8,128)(2,1)S(1)}, bf16[64,2048]{1,0:T(8,128)(2,1)S(1)}, u32[]{:S(2)}, u32[]{:S(2)}) collective-permute-start(bf16[64,2048]{1,0:T(8,128)(2,1)S(1)} %pad_maximum_fusion.5), channel_id=1, source_target_pairs={{0,2},{1,3},{2,0},{3,1},{4,6},{5,7},{6,4},{7,5},{8,10},{9,11},{10,... | collective-permute-start | bytes 786440 | tf_op jit(solution)/shard_map/ppermute | solution.py:84
  44.2 19.4 %collective-permute-start.23 = (bf16[128,2048]{1,0:T(8,128)(2,1)S(1)}, bf16[128,2048]{1,0:T(8,128)(2,1)S(1)}, u32[]{:S(2)}, u32[]{:S(2)}) collective-permute-start(bf16[128,2048]{1,0:T(8,128)(2,1)S(1)} %pad_maximum_fusion.2), channel_id=1, source_target_pairs={{0,2},{1,3},{2,0},{3,1},{4,6},{5,7},{6,4},{7,5},{8,10},{9,11},{10,... | collective-permute-start | bytes 1572872 | tf_op jit(solution)/shard_map/ppermute | solution.py:84
  45.5 18.3 %collective-permute-start.33 = (bf16[128,2048]{1,0:T(8,128)(2,1)S(1)}, bf16[128,2048]{1,0:T(8,128)(2,1)S(1)}, u32[]{:S(2)}, u32[]{:S(2)}) collective-permute-start(bf16[128,2048]{1,0:T(8,128)(2,1)S(1)} %pad_maximum_fusion.3), channel_id=1, source_target_pairs={{0,4},{1,5},{2,6},{3,7},{4,0},{5,1},{6,2},{7,3},{8,12},{9,13},{10,... | collective-permute-start | bytes 1572872 | tf_op jit(solution)/shard_map/ppermute | solution.py:84
  49.6 23.5 %collective-permute-start.3 = (bf16[128,2048]{1,0:T(8,128)(2,1)S(1)}, bf16[128,2048]{1,0:T(8,128)(2,1)S(1)}, u32[]{:S(2)}, u32[]{:S(2)}) collective-permute-start(bf16[128,2048]{1,0:T(8,128)(2,1)S(1)} %pad_maximum_fusion), channel_id=1, source_target_pairs={{0,2},{1,3},{2,0},{3,1},{4,6},{5,7},{6,4},{7,5},{8,10},{9,11},{10,... | collective-permute-start | bytes 1572872 | tf_op jit(solution)/shard_map/ppermute | solution.py:84
  52.4 20.8 %collective-permute-start.13 = (bf16[128,2048]{1,0:T(8,128)(2,1)S(1)}, bf16[128,2048]{1,0:T(8,128)(2,1)S(1)}, u32[]{:S(2)}, u32[]{:S(2)}) collective-permute-start(bf16[128,2048]{1,0:T(8,128)(2,1)S(1)} %pad_maximum_fusion.1), channel_id=1, source_target_pairs={{0,4},{1,5},{2,6},{3,7},{4,0},{5,1},{6,2},{7,3},{8,12},{9,13},{10,... | collective-permute-start | bytes 1572872 | tf_op jit(solution)/shard_map/ppermute | solution.py:84
  63.7 10.2 %collective-permute-start.24 = (bf16[256,2048]{1,0:T(8,128)(2,1)S(1)}, bf16[256,2048]{1,0:T(8,128)(2,1)S(1)}, u32[]{:S(2)}, u32[]{:S(2)}) collective-permute-start(bf16[256,2048]{1,0:T(8,128)(2,1)S(1)} %constant_dynamic-update-slice_fusion.10.near_ref), channel_id=1, source_target_pairs={{0,1},{1,0},{2,3},{3,2},{4,5},{5,4},{6,7},{7,6},{8,9},{9,8},{10,11... | collective-permute-start | bytes 3145736 | tf_op jit(solution)/shard_map/ppermute | solution.py:84
  63.9 23.0 %collective-permute-start.34 = (bf16[256,2048]{1,0:T(8,128)(2,1)S(1)}, bf16[256,2048]{1,0:T(8,128)(2,1)S(1)}, u32[]{:S(2)}, u32[]{:S(2)}) collective-permute-start(bf16[256,2048]{1,0:T(8,128)(2,1)S(1)} %constant_dynamic-update-slice_fusion.15.near_ref), channel_id=1, source_target_pairs={{0,1},{1,0},{2,3},{3,2},{4,5},{5,4},{6,7},{7,6},{8,9},{9,8},{10,11... | collective-permute-start | bytes 3145736 | tf_op jit(solution)/shard_map/ppermute | solution.py:84
  73.2 27.0 %collective-permute-start.4 = (bf16[256,2048]{1,0:T(8,128)(2,1)S(1)}, bf16[256,2048]{1,0:T(8,128)(2,1)}, u32[]{:S(2)}, u32[]{:S(2)}) collective-permute-start(bf16[256,2048]{1,0:T(8,128)(2,1)S(1)} %constant_dynamic-update-slice_fusion.near_ref), channel_id=1, source_target_pairs={{0,1},{1,0},{2,3},{3,2},{4,5},{5,4},{6,7},{7,6},{8,9},{9,8},{10,11... | collective-permute-start | bytes 3145736 | tf_op jit(solution)/shard_map/ppermute | solution.py:84
  73.3 38.8 %collective-permute-start.14 = (bf16[256,2048]{1,0:T(8,128)(2,1)S(1)}, bf16[256,2048]{1,0:T(8,128)(2,1)S(1)}, u32[]{:S(2)}, u32[]{:S(2)}) collective-permute-start(bf16[256,2048]{1,0:T(8,128)(2,1)S(1)} %constant_dynamic-update-slice_fusion.5.near_ref), channel_id=1, source_target_pairs={{0,1},{1,0},{2,3},{3,2},{4,5},{5,4},{6,7},{7,6},{8,9},{9,8},{10,11... | collective-permute-start | bytes 3145736 | tf_op jit(solution)/shard_map/ppermute | solution.py:84
  86.7 38.6 %collective-permute-start.25 = (bf16[256,2048]{1,0:T(8,128)(2,1)}, bf16[256,2048]{1,0:T(8,128)(2,1)S(1)}, u32[]{:S(2)}, u32[]{:S(2)}) collective-permute-start(bf16[256,2048]{1,0:T(8,128)(2,1)} %get-tuple-element.19), channel_id=1, source_target_pairs={{0,1},{1,0},{2,3},{3,2},{4,5},{5,4},{6,7},{7,6},{8,9},{9,8},{10,11... | collective-permute-start | bytes 3145736 | tf_op jit(solution)/shard_map/ppermute | solution.py:84
  99.8 27.1 %collective-permute-start.35 = (bf16[256,2048]{1,0:T(8,128)(2,1)}, bf16[256,2048]{1,0:T(8,128)(2,1)S(1)}, u32[]{:S(2)}, u32[]{:S(2)}) collective-permute-start(bf16[256,2048]{1,0:T(8,128)(2,1)} %get-tuple-element.21), channel_id=1, source_target_pairs={{0,1},{1,0},{2,3},{3,2},{4,5},{5,4},{6,7},{7,6},{8,9},{9,8},{10,11... | collective-permute-start | bytes 3145736 | tf_op jit(solution)/shard_map/ppermute | solution.py:84
  112.0 16.8 %collective-permute-start.5 = (bf16[256,2048]{1,0:T(8,128)(2,1)}, bf16[256,2048]{1,0:T(8,128)(2,1)S(1)}, u32[]{:S(2)}, u32[]{:S(2)}) collective-permute-start(bf16[256,2048]{1,0:T(8,128)(2,1)} %get-tuple-element.15), channel_id=1, source_target_pairs={{0,1},{1,0},{2,3},{3,2},{4,5},{5,4},{6,7},{7,6},{8,9},{9,8},{10,11... | collective-permute-start | bytes 3145736 | tf_op jit(solution)/shard_map/ppermute | solution.py:84
  125.8 14.8 %collective-permute-start.26 = (bf16[128,2048]{1,0:T(8,128)(2,1)S(1)}, bf16[128,2048]{1,0:T(8,128)(2,1)S(1)}, u32[]{:S(2)}, u32[]{:S(2)}) collective-permute-start(bf16[128,2048]{1,0:T(8,128)(2,1)S(1)} %slice.255), channel_id=1, source_target_pairs={{0,2},{1,3},{2,0},{3,1},{4,6},{5,7},{6,4},{7,5},{8,10},{9,11},{10,... | collective-permute-start | bytes 1572872 | tf_op jit(solution)/shard_map/ppermute | solution.py:84
  127.3 14.9 %collective-permute-start.36 = (bf16[128,2048]{1,0:T(8,128)(2,1)S(1)}, bf16[128,2048]{1,0:T(8,128)(2,1)S(1)}, u32[]{:S(2)}, u32[]{:S(2)}) collective-permute-start(bf16[128,2048]{1,0:T(8,128)(2,1)S(1)} %slice.267), channel_id=1, source_target_pairs={{0,4},{1,5},{2,6},{3,7},{4,0},{5,1},{6,2},{7,3},{8,12},{9,13},{10,... | collective-permute-start | bytes 1572872 | tf_op jit(solution)/shard_map/ppermute | solution.py:84
  129.2 22.6 %collective-permute-start.6 = (bf16[128,2048]{1,0:T(8,128)(2,1)S(1)}, bf16[128,2048]{1,0:T(8,128)(2,1)S(1)}, u32[]{:S(2)}, u32[]{:S(2)}) collective-permute-start(bf16[128,2048]{1,0:T(8,128)(2,1)S(1)} %slice.231), channel_id=1, source_target_pairs={{0,2},{1,3},{2,0},{3,1},{4,6},{5,7},{6,4},{7,5},{8,10},{9,11},{10,... | collective-permute-start | bytes 1572872 | tf_op jit(solution)/shard_map/ppermute | solution.py:84
  130.4 23.1 %collective-permute-start.16 = (bf16[128,2048]{1,0:T(8,128)(2,1)S(1)}, bf16[128,2048]{1,0:T(8,128)(2,1)S(1)}, u32[]{:S(2)}, u32[]{:S(2)}) collective-permute-start(bf16[128,2048]{1,0:T(8,128)(2,1)S(1)} %slice.243), channel_id=1, source_target_pairs={{0,4},{1,5},{2,6},{3,7},{4,0},{5,1},{6,2},{7,3},{8,12},{9,13},{10,... | collective-permute-start | bytes 1572872 | tf_op jit(solution)/shard_map/ppermute | solution.py:84
  140.8 18.3 %collective-permute-start.27 = (bf16[64,2048]{1,0:T(8,128)(2,1)S(1)}, bf16[64,2048]{1,0:T(8,128)(2,1)S(1)}, u32[]{:S(2)}, u32[]{:S(2)}) collective-permute-start(bf16[64,2048]{1,0:T(8,128)(2,1)S(1)} %slice.257), channel_id=1, source_target_pairs={{0,4},{1,5},{2,6},{3,7},{4,0},{5,1},{6,2},{7,3},{8,12},{9,13},{10,... | collective-permute-start | bytes 786440 | tf_op jit(solution)/shard_map/ppermute | solution.py:84
  142.4 17.8 %collective-permute-start.37 = (bf16[64,2048]{1,0:T(8,128)(2,1)S(1)}, bf16[64,2048]{1,0:T(8,128)(2,1)S(1)}, u32[]{:S(2)}, u32[]{:S(2)}) collective-permute-start(bf16[64,2048]{1,0:T(8,128)(2,1)S(1)} %slice.269), channel_id=1, source_target_pairs={{0,2},{1,3},{2,0},{3,1},{4,6},{5,7},{6,4},{7,5},{8,10},{9,11},{10,... | collective-permute-start | bytes 786440 | tf_op jit(solution)/shard_map/ppermute | solution.py:84
  152.0 11.5 %collective-permute-start.7 = (bf16[64,2048]{1,0:T(8,128)(2,1)S(1)}, bf16[64,2048]{1,0:T(8,128)(2,1)S(1)}, u32[]{:S(2)}, u32[]{:S(2)}) collective-permute-start(bf16[64,2048]{1,0:T(8,128)(2,1)S(1)} %slice.233), channel_id=1, source_target_pairs={{0,4},{1,5},{2,6},{3,7},{4,0},{5,1},{6,2},{7,3},{8,12},{9,13},{10,... | collective-permute-start | bytes 786440 | tf_op jit(solution)/shard_map/ppermute | solution.py:84
  153.6 11.0 %collective-permute-start.17 = (bf16[64,2048]{1,0:T(8,128)(2,1)S(1)}, bf16[64,2048]{1,0:T(8,128)(2,1)S(1)}, u32[]{:S(2)}, u32[]{:S(2)}) collective-permute-start(bf16[64,2048]{1,0:T(8,128)(2,1)S(1)} %slice.245), channel_id=1, source_target_pairs={{0,2},{1,3},{2,0},{3,1},{4,6},{5,7},{6,4},{7,5},{8,10},{9,11},{10,... | collective-permute-start | bytes 786440 | tf_op jit(solution)/shard_map/ppermute | solution.py:84
  163.6 9.2 %collective-permute-start.8 = (bf16[32,2048]{1,0:T(8,128)(2,1)S(1)}, bf16[32,2048]{1,0:T(8,128)(2,1)S(1)}, u32[]{:S(2)}, u32[]{:S(2)}) collective-permute-start(bf16[32,2048]{1,0:T(8,128)(2,1)S(1)} %slice.235), channel_id=1, source_target_pairs={{0,8},{1,9},{2,10},{3,11},{4,12},{5,13},{6,14},{7,15},{8,0},{9,1},... | collective-permute-start | bytes 393224 | tf_op jit(solution)/shard_map/ppermute | solution.py:84
  164.7 10.0 %collective-permute-start.18 = (bf16[32,2048]{1,0:T(8,128)(2,1)S(1)}, bf16[32,2048]{1,0:T(8,128)(2,1)S(1)}, u32[]{:S(2)}, u32[]{:S(2)}) collective-permute-start(bf16[32,2048]{1,0:T(8,128)(2,1)S(1)} %slice.247), channel_id=1, source_target_pairs={{0,8},{1,9},{2,10},{3,11},{4,12},{5,13},{6,14},{7,15},{8,0},{9,1},... | collective-permute-start | bytes 393224 | tf_op jit(solution)/shard_map/ppermute | solution.py:84
  165.9 10.0 %collective-permute-start.29 = (bf16[16,2048]{1,0:T(8,128)(2,1)S(1)}, bf16[16,2048]{1,0:T(8,128)(2,1)S(1)}, u32[]{:S(2)}, u32[]{:S(2)}) collective-permute-start(bf16[16,2048]{1,0:T(8,128)(2,1)S(1)} %slice.261), channel_id=1, source_target_pairs={{0,16},{1,17},{2,18},{3,19},{4,20},{5,21},{6,22},{7,23},{8,24},{9,... | collective-permute-start | bytes 196616 | tf_op jit(solution)/shard_map/ppermute | solution.py:84
  (32 other events, 239.5 us)

commit v4 on v3

--- a/solution.py
+++ b/solution.py
@@ -185,22 +185,40 @@
         streams.append(stream)
         for side, order in enumerate(orders):
             parts.append((micro, side, order, normed[side * half : (side + 1) * half]))
+    outs = {}
+    marks = []
+    for micro in range(micro_count):
+        sides = [part for part in parts if part[0] == micro]
+        bufs = [part[3] for part in sides]
+        fars = [None, None]
+        for step in range(bits):
+            behind = step - max(bits - 3, 0)
+            for _, side, order, _ in sides:
+                buf = bufs[side]
+                if micro > 0 and behind >= 0:
+                    buf = lax.optimization_barrier((buf, *marks[min(behind, 2)]))[0]
+                got = swap(buf, order[step], shards)
+                if step == bits - 1:
+                    bufs[side], fars[side] = buf, got
+                else:
+                    bufs[side] = jnp.concatenate([buf, got], axis=0)
+        marks = [tuple(fars)]
+        for _, side, order, _ in sides:
+            spread = [0]
+            for bit in order:
+                spread = spread + [k ^ (1 << bit) for k in spread]
+            weight = jnp.take(
+                mine[micro, :, side * half : (side + 1) * half],
+                jnp.bitwise_xor(me, jnp.array(spread, dtype=jnp.int32)),
+                axis=0,
+            ).reshape(2, -1, 1)
+            outs[micro, side] = weighted_rows(
+                bufs[side], fars[side], weight[0], weight[1], gate_proj, up_proj, down_proj
+            )
+            marks.append((outs[micro, side][0],))
     sums = {}
-    for micro, side, order, buf in parts:
-        spread = [0]
-        for bit in order:
-            spread = spread + [k ^ (1 << bit) for k in spread]
-        weight = jnp.take(
-            mine[micro, :, side * half : (side + 1) * half],
-            jnp.bitwise_xor(me, jnp.array(spread, dtype=jnp.int32)),
-            axis=0,
-        ).reshape(2, -1, 1)
-        for bit in order[:-1]:
-            buf = jnp.concatenate([buf, swap(buf, bit, shards)], axis=0)
-        far = swap(buf, order[-1], shards)
-        near_out, far_out = weighted_rows(
-            buf, far, weight[0], weight[1], gate_proj, up_proj, down_proj
-        )
+    for micro, side, order, _ in parts:
+        near_out, far_out = outs[micro, side]
         acc = wide_sum(near_out, swap(far_out, order[-1], shards))
         for bit in order[-2::-1]:
             keep = acc.shape[0] // 2

time: 182 us -> 209 us (1.15)
  waiting for transfers between devices: 65 us -> 80.3 us
  other arithmetic: 3.89 us -> 11.1 us
  starting transfers between devices: 45.1 us -> 48.3 us
    ppermute x40, waiting for transfers between devices: 64.2 us -> 80.3 us  [swap(): return lax.ppermute(x, 'ex', [(i, i ^ 1 << bit) for i in range(shards)])]
    all_to_all x1, starting transfers between devices: 3.82 us -> 7.3 us  [on_device(): mine = lax.all_to_all(table, 'ex', split_axis=2, concat_axis=1, tiled=True)]
    concatenate x12 -> x14, other arithmetic: 0.28 us -> 3.23 us  [on_device(): bufs[side] = jnp.concatenate([buf, got], axis=0)]
    convert_element_type x16, other arithmetic: 2.45 us -> 5.26 us  [wide_sum(): return (a.astype(jnp.float32) + b.astype(jnp.float32)).astype(jnp.bfloat16)]
    unnamed x60 -> x50, local copies, waits for them, and re-layouts: 10.9 us -> 10.8 us
  transfers between devices with their start and end apart: 41 -> 41, of which waited for: 19 -> 22; matrix products, arithmetic and copies ran while one was open for 6% -> 9% of each run, Pallas kernels for 26% -> 24%
where the time goes in v4:
time: 209 us; the launch traced here: 208 us
  waiting for transfers between devices  80.3 us (38%)
  Pallas kernels  49.6 us (24%)
  starting transfers between devices  48.3 us (23%)
  local copies, waits for them, and re-layouts  18.1 us (9%)
  other arithmetic  11.1 us (5%)
    ppermute x40, waiting for transfers between devices, swap(): return lax.ppermute(x, 'ex', [(i, i ^ 1 << bit) for i in range(shards)])  80.3 us
    pallas_call x4, Pallas kernels, weighted_rows(): pl.pallas_call(expert_kernel, out_shape=[jax.ShapeDtypeStruct((rows, widt...  47.4 us
    ppermute x40, starting transfers between devices, swap(): return lax.ppermute(x, 'ex', [(i, i ^ 1 << bit) for i in range(shards)])  41 us
    unnamed x50, local copies, waits for them, and re-layouts  10.8 us
    all_to_all x1, starting transfers between devices, on_device(): mine = lax.all_to_all(table, 'ex', split_axis=2, concat_axis=1, tiled=True)  7.3 us
    convert_element_type x16, other arithmetic, wide_sum(): return (a.astype(jnp.float32) + b.astype(jnp.float32)).astype(jnp.bfloat16)  5.26 us
  transfers between devices with their start and end apart: 41, of which 22 were waited for; matrix products, arithmetic and copies ran while one was open for 9% of the time, Pallas kernels for 24%

profile of v4, /device:TPU:0, one launch (start us, length us, event | category | flops | bytes accessed | tf_op | source)
XLA Modules:
  0.0 208.2 jit_solution(2617380205999876882)
XLA Ops:
  3.2 7.3 %all-to-all-start = ((f32[2,32,32]{1,0,2:T(2,128)}), f32[2,32,32]{1,0,2:T(2,128)S(1)}, u32[]{:S(2)}, u32[]{:S(2)}) async-start(f32[2,32,32]{1,0,2:T(2,128)} %copy.50), calls=%async_computation | async-start | bytes 65536 | tf_op jit(solution)/shard_map/all_to_all | solution.py:167
  19.2 2.7 %collective-permute-start.20 = (bf16[16,2048]{1,0:T(8,128)(2,1)S(1)}, bf16[16,2048]{1,0:T(8,128)(2,1)S(1)}, u32[]{:S(2)}, u32[]{:S(2)}) collective-permute-start(bf16[16,2048]{1,0:T(8,128)(2,1)S(1)} %get-tuple-element.44), channel_id=1, source_target_pairs={{0,16},{1,17},{2,18},{3,19},{4,20},{5,21},{6,22},{7,23},{8,24},{9,... | collective-permute-start | bytes 196616 | tf_op jit(solution)/shard_map/ppermute | solution.py:84
  22.8 2.7 %collective-permute-start.10 = (bf16[16,2048]{1,0:T(8,128)(2,1)S(1)}, bf16[16,2048]{1,0:T(8,128)(2,1)S(1)}, u32[]{:S(2)}, u32[]{:S(2)}) collective-permute-start(bf16[16,2048]{1,0:T(8,128)(2,1)S(1)} %get-tuple-element.46), channel_id=1, source_target_pairs={{0,16},{1,17},{2,18},{3,19},{4,20},{5,21},{6,22},{7,23},{8,24},{9,... | collective-permute-start | bytes 196616 | tf_op jit(solution)/shard_map/ppermute | solution.py:84
  30.3 1.8 collective-permute-start.21
  36.3 3.6 %collective-permute-done.11 = bf16[32,2048]{1,0:T(8,128)(2,1)S(1)} collective-permute-done((bf16[32,2048]{1,0:T(8,128)(2,1)S(1)}, bf16[32,2048]{1,0:T(8,128)(2,1)S(1)}, u32[]{:S(2)}, u32[]{:S(2)}) %collective-permute-start.11) | collective-permute-done | bytes 131104 | tf_op jit(solution)/shard_map/ppermute | solution.py:84
  40.0 1.8 collective-permute-start.12
  42.7 1.8 collective-permute-start.2
  45.2 3.0 %collective-permute-done.12 = bf16[64,2048]{1,0:T(8,128)(2,1)S(1)} collective-permute-done((bf16[64,2048]{1,0:T(8,128)(2,1)S(1)}, bf16[64,2048]{1,0:T(8,128)(2,1)S(1)}, u32[]{:S(2)}, u32[]{:S(2)}) %collective-permute-start.12) | collective-permute-done | bytes 262176 | tf_op jit(solution)/shard_map/ppermute | solution.py:84
  48.3 1.8 collective-permute-start.13
  50.1 1.9 collective-permute-done.2
  52.0 1.8 collective-permute-start.3
  53.8 8.4 %collective-permute-done.13 = bf16[128,2048]{1,0:T(8,128)(2,1)S(1)} collective-permute-done((bf16[128,2048]{1,0:T(8,128)(2,1)S(1)}, bf16[128,2048]{1,0:T(8,128)(2,1)S(1)}, u32[]{:S(2)}, u32[]{:S(2)}) %collective-permute-start.13) | collective-permute-done | bytes 524320 | tf_op jit(solution)/shard_map/ppermute | solution.py:84
  64.4 5.8 %collective-permute-done.31 = bf16[32,2048]{1,0:T(8,128)(2,1)S(1)} collective-permute-done((bf16[32,2048]{1,0:T(8,128)(2,1)S(1)}, bf16[32,2048]{1,0:T(8,128)(2,1)S(1)}, u32[]{:S(2)}, u32[]{:S(2)}) %collective-permute-start.31) | collective-permute-done | bytes 131104 | tf_op jit(solution)/shard_map/ppermute | solution.py:84
  72.0 11.9 %shard_map.165 = (bf16[256,2048]{1,0:T(8,128)(2,1)S(1)}, bf16[256,2048]{1,0:T(8,128)(2,1)}) custom-call(bf16[256,2048]{1,0:T(8,128)(2,1)} %copy-done.11, bf16[256,2048]{1,0:T(8,128)(2,1)} %copy-done.18, f32[256,1]{1,0:T(8,128)S(1)} %squeeze.54.near_w, f32[256,1]{1,0:T(8,128)S(1)} %squeeze.55.far_w, bf16[1,2048,768]{2,1,0:T(8,128)(2,1)} %gate_ref.7, ...), custom_call_target="tpu_custom_call" | custom-call | flops 4831838208 | bytes 13631488 | tf_op jit(solution)/shard_map/pallas_call | solution.py:119
  83.9 1.8 collective-permute-start.22
  87.1 11.8 %shard_map.164 = (bf16[256,2048]{1,0:T(8,128)(2,1)S(1)}, bf16[256,2048]{1,0:T(8,128)(2,1)}) custom-call(bf16[256,2048]{1,0:T(8,128)(2,1)} %copy-done.9, bf16[256,2048]{1,0:T(8,128)(2,1)} %copy-done.16, f32[256,1]{1,0:T(8,128)S(1)} %squeeze.52.near_w, f32[256,1]{1,0:T(8,128)S(1)} %squeeze.53.far_w, bf16[1,2048,768]{2,1,0:T(8,128)(2,1)} %gate_ref.7, ...), custom_call_target="tpu_custom_call" | custom-call | flops 4831838208 | bytes 13631488 | tf_op jit(solution)/shard_map/pallas_call | solution.py:119
  101.8 11.1 %collective-permute-done.23 = bf16[128,2048]{1,0:T(8,128)(2,1)} collective-permute-done((bf16[128,2048]{1,0:T(8,128)(2,1)S(1)}, bf16[128,2048]{1,0:T(8,128)(2,1)}, u32[]{:S(2)}, u32[]{:S(2)}) %collective-permute-start.23) | collective-permute-done | bytes 524320 | tf_op jit(solution)/shard_map/ppermute | solution.py:84
  114.0 2.0 add_convert_fusion.2
  120.1 8.9 %collective-permute-done.16 = bf16[128,2048]{1,0:T(8,128)(2,1)S(1)} collective-permute-done((bf16[128,2048]{1,0:T(8,128)(2,1)S(1)}, bf16[128,2048]{1,0:T(8,128)(2,1)S(1)}, u32[]{:S(2)}, u32[]{:S(2)}) %collective-permute-start.16) | collective-permute-done | bytes 524320 | tf_op jit(solution)/shard_map/ppermute | solution.py:84
  129.8 2.2 %collective-permute-done.6 = bf16[128,2048]{1,0:T(8,128)(2,1)S(1)} collective-permute-done((bf16[128,2048]{1,0:T(8,128)(2,1)S(1)}, bf16[128,2048]{1,0:T(8,128)(2,1)S(1)}, u32[]{:S(2)}, u32[]{:S(2)}) %collective-permute-start.6) | collective-permute-done | bytes 524320 | tf_op jit(solution)/shard_map/ppermute | solution.py:84
  133.9 2.7 %collective-permute-done.17 = bf16[64,2048]{1,0:T(8,128)(2,1)S(1)} collective-permute-done((bf16[64,2048]{1,0:T(8,128)(2,1)S(1)}, bf16[64,2048]{1,0:T(8,128)(2,1)S(1)}, u32[]{:S(2)}, u32[]{:S(2)}) %collective-permute-start.17) | collective-permute-done | bytes 262176 | tf_op jit(solution)/shard_map/ppermute | solution.py:84
  138.0 11.9 %shard_map.168 = (bf16[256,2048]{1,0:T(8,128)(2,1)S(1)}, bf16[256,2048]{1,0:T(8,128)(2,1)}) custom-call(bf16[256,2048]{1,0:T(8,128)(2,1)} %copy-done.5, bf16[256,2048]{1,0:T(8,128)(2,1)} %copy-done.17, f32[256,1]{1,0:T(8,128)S(1)} %squeeze.58.near_w, f32[256,1]{1,0:T(8,128)S(1)} %squeeze.59.far_w, bf16[1,2048,768]{2,1,0:T(8,128)(2,1)} %gate_ref.7, ...), custom_call_target="tpu_custom_call" | custom-call | flops 4831838208 | bytes 13631488 | tf_op jit(solution)/shard_map/pallas_call | solution.py:119
  150.9 11.8 %shard_map.167 = (bf16[256,2048]{1,0:T(8,128)(2,1)S(1)}, bf16[256,2048]{1,0:T(8,128)(2,1)}) custom-call(bf16[256,2048]{1,0:T(8,128)(2,1)} %copy-done.4, bf16[256,2048]{1,0:T(8,128)(2,1)} %copy-done.15, f32[256,1]{1,0:T(8,128)S(1)} %squeeze.56.near_w, f32[256,1]{1,0:T(8,128)S(1)} %squeeze.57.far_w, bf16[1,2048,768]{2,1,0:T(8,128)(2,1)} %gate_ref.7, ...), custom_call_target="tpu_custom_call" | custom-call | flops 4831838208 | bytes 13631488 | tf_op jit(solution)/shard_map/pallas_call | solution.py:119
  163.3 1.8 collective-permute-start.8
  165.2 2.1 collective-permute-start.19
  167.2 2.3 %collective-permute-done.8 = bf16[32,2048]{1,0:T(8,128)(2,1)S(1)} collective-permute-done((bf16[32,2048]{1,0:T(8,128)(2,1)S(1)}, bf16[32,2048]{1,0:T(8,128)(2,1)S(1)}, u32[]{:S(2)}, u32[]{:S(2)}) %collective-permute-start.8) | collective-permute-done | bytes 131104 | tf_op jit(solution)/shard_map/ppermute | solution.py:84
  169.5 3.5 %collective-permute-start.9 = (bf16[16,2048]{1,0:T(8,128)(2,1)S(1)}, bf16[16,2048]{1,0:T(8,128)(2,1)S(1)}, u32[]{:S(2)}, u32[]{:S(2)}) collective-permute-start(bf16[16,2048]{1,0:T(8,128)(2,1)S(1)} %slice.237), channel_id=1, source_target_pairs={{0,16},{1,17},{2,18},{3,19},{4,20},{5,21},{6,22},{7,23},{8,24},{9,... | collective-permute-start | bytes 196616 | tf_op jit(solution)/shard_map/ppermute | solution.py:84
  176.1 9.4 %collective-permute-done.36 = bf16[128,2048]{1,0:T(8,128)(2,1)S(1)} collective-permute-done((bf16[128,2048]{1,0:T(8,128)(2,1)S(1)}, bf16[128,2048]{1,0:T(8,128)(2,1)S(1)}, u32[]{:S(2)}, u32[]{:S(2)}) %collective-permute-start.36) | collective-permute-done | bytes 524320 | tf_op jit(solution)/shard_map/ppermute | solution.py:84
  189.1 3.8 %collective-permute-done.37 = bf16[64,2048]{1,0:T(8,128)(2,1)S(1)} collective-permute-done((bf16[64,2048]{1,0:T(8,128)(2,1)S(1)}, bf16[64,2048]{1,0:T(8,128)(2,1)S(1)}, u32[]{:S(2)}, u32[]{:S(2)}) %collective-permute-start.37) | collective-permute-done | bytes 262176 | tf_op jit(solution)/shard_map/ppermute | solution.py:84
  198.8 2.5 %collective-permute-done.28 = bf16[32,2048]{1,0:T(8,128)(2,1)S(1)} collective-permute-done((bf16[32,2048]{1,0:T(8,128)(2,1)S(1)}, bf16[32,2048]{1,0:T(8,128)(2,1)S(1)}, u32[]{:S(2)}, u32[]{:S(2)}) %collective-permute-start.28) | collective-permute-done | bytes 131104 | tf_op jit(solution)/shard_map/ppermute | solution.py:84
  201.4 1.9 collective-permute-done.39
  203.3 3.9 %collective-permute-done.29 = bf16[16,2048]{1,0:T(8,128)(2,1)S(1)} collective-permute-done((bf16[16,2048]{1,0:T(8,128)(2,1)S(1)}, bf16[16,2048]{1,0:T(8,128)(2,1)S(1)}, u32[]{:S(2)}, u32[]{:S(2)}) %collective-permute-start.29) | collective-permute-done | bytes 65568 | tf_op jit(solution)/shard_map/ppermute | solution.py:84
  (199 shorter events, 55.5 us)
Async XLA Ops:
  3.2 24.1 %all-to-all-start = ((f32[2,32,32]{1,0,2:T(2,128)}), f32[2,32,32]{1,0,2:T(2,128)S(1)}, u32[]{:S(2)}, u32[]{:S(2)}) async-start(f32[2,32,32]{1,0,2:T(2,128)} %copy.50), calls=%async_computation | async-start | bytes 65536 | tf_op jit(solution)/shard_map/all_to_all | solution.py:167
  19.2 11.1 %collective-permute-start.20 = (bf16[16,2048]{1,0:T(8,128)(2,1)S(1)}, bf16[16,2048]{1,0:T(8,128)(2,1)S(1)}, u32[]{:S(2)}, u32[]{:S(2)}) collective-permute-start(bf16[16,2048]{1,0:T(8,128)(2,1)S(1)} %get-tuple-element.44), channel_id=1, source_target_pairs={{0,16},{1,17},{2,18},{3,19},{4,20},{5,21},{6,22},{7,23},{8,24},{9,... | collective-permute-start | bytes 196616 | tf_op jit(solution)/shard_map/ppermute | solution.py:84
  21.9 42.4 %collective-permute-start.30 = (bf16[16,2048]{1,0:T(8,128)(2,1)S(1)}, bf16[16,2048]{1,0:T(8,128)(2,1)S(1)}, u32[]{:S(2)}, u32[]{:S(2)}) collective-permute-start(bf16[16,2048]{1,0:T(8,128)(2,1)S(1)} %get-tuple-element.45), channel_id=1, source_target_pairs={{0,16},{1,17},{2,18},{3,19},{4,20},{5,21},{6,22},{7,23},{8,24},{9,... | collective-permute-start | bytes 196616 | tf_op jit(solution)/shard_map/ppermute | solution.py:84
  22.8 10.6 %collective-permute-start.10 = (bf16[16,2048]{1,0:T(8,128)(2,1)S(1)}, bf16[16,2048]{1,0:T(8,128)(2,1)S(1)}, u32[]{:S(2)}, u32[]{:S(2)}) collective-permute-start(bf16[16,2048]{1,0:T(8,128)(2,1)S(1)} %get-tuple-element.46), channel_id=1, source_target_pairs={{0,16},{1,17},{2,18},{3,19},{4,20},{5,21},{6,22},{7,23},{8,24},{9,... | collective-permute-start | bytes 196616 | tf_op jit(solution)/shard_map/ppermute | solution.py:84
  25.5 8.9 %collective-permute-start = (bf16[16,2048]{1,0:T(8,128)(2,1)S(1)}, bf16[16,2048]{1,0:T(8,128)(2,1)S(1)}, u32[]{:S(2)}, u32[]{:S(2)}) collective-permute-start(bf16[16,2048]{1,0:T(8,128)(2,1)S(1)} %get-tuple-element.49), channel_id=1, source_target_pairs={{0,16},{1,17},{2,18},{3,19},{4,20},{5,21},{6,22},{7,23},{8,24},{9,... | collective-permute-start | bytes 196616 | tf_op jit(solution)/shard_map/ppermute | solution.py:84
  30.3 34.1 %collective-permute-start.21 = (bf16[32,2048]{1,0:T(8,128)(2,1)S(1)}, bf16[32,2048]{1,0:T(8,128)(2,1)S(1)}, u32[]{:S(2)}, u32[]{:S(2)}) collective-permute-start(bf16[32,2048]{1,0:T(8,128)(2,1)S(1)} %pad_maximum_fusion.13), channel_id=1, source_target_pairs={{0,8},{1,9},{2,10},{3,11},{4,12},{5,13},{6,14},{7,15},{8,0},{9,1},... | collective-permute-start | bytes 393224 | tf_op jit(solution)/shard_map/ppermute | solution.py:84
  34.4 8.3 %collective-permute-start.1 = (bf16[32,2048]{1,0:T(8,128)(2,1)S(1)}, bf16[32,2048]{1,0:T(8,128)(2,1)S(1)}, u32[]{:S(2)}, u32[]{:S(2)}) collective-permute-start(bf16[32,2048]{1,0:T(8,128)(2,1)S(1)} %pad_maximum_fusion.11), channel_id=1, source_target_pairs={{0,8},{1,9},{2,10},{3,11},{4,12},{5,13},{6,14},{7,15},{8,0},{9,1},... | collective-permute-start | bytes 393224 | tf_op jit(solution)/shard_map/ppermute | solution.py:84
  40.0 8.2 %collective-permute-start.12 = (bf16[64,2048]{1,0:T(8,128)(2,1)S(1)}, bf16[64,2048]{1,0:T(8,128)(2,1)S(1)}, u32[]{:S(2)}, u32[]{:S(2)}) collective-permute-start(bf16[64,2048]{1,0:T(8,128)(2,1)S(1)} %pad_maximum_fusion.7), channel_id=1, source_target_pairs={{0,2},{1,3},{2,0},{3,1},{4,6},{5,7},{6,4},{7,5},{8,10},{9,11},{10,... | collective-permute-start | bytes 786440 | tf_op jit(solution)/shard_map/ppermute | solution.py:84
  42.7 9.2 %collective-permute-start.2 = (bf16[64,2048]{1,0:T(8,128)(2,1)S(1)}, bf16[64,2048]{1,0:T(8,128)(2,1)S(1)}, u32[]{:S(2)}, u32[]{:S(2)}) collective-permute-start(bf16[64,2048]{1,0:T(8,128)(2,1)S(1)} %pad_maximum_fusion.6), channel_id=1, source_target_pairs={{0,4},{1,5},{2,6},{3,7},{4,0},{5,1},{6,2},{7,3},{8,12},{9,13},{10,... | collective-permute-start | bytes 786440 | tf_op jit(solution)/shard_map/ppermute | solution.py:84
  48.3 14.0 %collective-permute-start.13 = (bf16[128,2048]{1,0:T(8,128)(2,1)S(1)}, bf16[128,2048]{1,0:T(8,128)(2,1)S(1)}, u32[]{:S(2)}, u32[]{:S(2)}) collective-permute-start(bf16[128,2048]{1,0:T(8,128)(2,1)S(1)} %pad_maximum_fusion.3), channel_id=1, source_target_pairs={{0,4},{1,5},{2,6},{3,7},{4,0},{5,1},{6,2},{7,3},{8,12},{9,13},{10,... | collective-permute-start | bytes 1572872 | tf_op jit(solution)/shard_map/ppermute | solution.py:84
  52.0 12.2 %collective-permute-start.3 = (bf16[128,2048]{1,0:T(8,128)(2,1)S(1)}, bf16[128,2048]{1,0:T(8,128)(2,1)S(1)}, u32[]{:S(2)}, u32[]{:S(2)}) collective-permute-start(bf16[128,2048]{1,0:T(8,128)(2,1)S(1)} %pad_maximum_fusion.2), channel_id=1, source_target_pairs={{0,2},{1,3},{2,0},{3,1},{4,6},{5,7},{6,4},{7,5},{8,10},{9,11},{10,... | collective-permute-start | bytes 1572872 | tf_op jit(solution)/shard_map/ppermute | solution.py:84
  62.3 8.7 %collective-permute-start.14 = (bf16[256,2048]{1,0:T(8,128)(2,1)S(1)}, bf16[256,2048]{1,0:T(8,128)(2,1)S(1)}, u32[]{:S(2)}, u32[]{:S(2)}) collective-permute-start(bf16[256,2048]{1,0:T(8,128)(2,1)S(1)} %constant_dynamic-update-slice_fusion.5.near_ref), channel_id=1, source_target_pairs={{0,1},{1,0},{2,3},{3,2},{4,5},{5,4},{6,7},{7,6},{8,9},{9,8},{10,11... | collective-permute-start | bytes 3145736 | tf_op jit(solution)/shard_map/ppermute | solution.py:84
  64.2 19.7 %collective-permute-start.4 = (bf16[256,2048]{1,0:T(8,128)(2,1)S(1)}, bf16[256,2048]{1,0:T(8,128)(2,1)S(1)}, u32[]{:S(2)}, u32[]{:S(2)}) collective-permute-start(bf16[256,2048]{1,0:T(8,128)(2,1)S(1)} %constant_dynamic-update-slice_fusion.near_ref), channel_id=1, source_target_pairs={{0,1},{1,0},{2,3},{3,2},{4,5},{5,4},{6,7},{7,6},{8,9},{9,8},{10,11... | collective-permute-start | bytes 3145736 | tf_op jit(solution)/shard_map/ppermute | solution.py:84
  83.9 30.2 %collective-permute-start.15 = (bf16[256,2048]{1,0:T(8,128)(2,1)}, bf16[256,2048]{1,0:T(8,128)(2,1)}, u32[]{:S(2)}, u32[]{:S(2)}) collective-permute-start(bf16[256,2048]{1,0:T(8,128)(2,1)} %get-tuple-element.23), channel_id=1, source_target_pairs={{0,1},{1,0},{2,3},{3,2},{4,5},{5,4},{6,7},{7,6},{8,9},{9,8},{10,11... | collective-permute-start | bytes 3145736 | tf_op jit(solution)/shard_map/ppermute | solution.py:84
  83.9 15.1 %collective-permute-start.22 = (bf16[64,2048]{1,0:T(8,128)(2,1)S(1)}, bf16[64,2048]{1,0:T(8,128)(2,1)S(1)}, u32[]{:S(2)}, u32[]{:S(2)}) collective-permute-start(bf16[64,2048]{1,0:T(8,128)(2,1)S(1)} %pad_maximum_fusion.8), channel_id=1, source_target_pairs={{0,4},{1,5},{2,6},{3,7},{4,0},{5,1},{6,2},{7,3},{8,12},{9,13},{10,... | collective-permute-start | bytes 786440 | tf_op jit(solution)/shard_map/ppermute | solution.py:84
  85.7 14.4 %collective-permute-start.32 = (bf16[64,2048]{1,0:T(8,128)(2,1)}, bf16[64,2048]{1,0:T(8,128)(2,1)}, u32[]{:S(2)}, u32[]{:S(2)}) collective-permute-start(bf16[64,2048]{1,0:T(8,128)(2,1)} %pad_maximum_fusion.9), channel_id=1, source_target_pairs={{0,2},{1,3},{2,0},{3,1},{4,6},{5,7},{6,4},{7,5},{8,10},{9,11},{10,... | collective-permute-start | bytes 786440 | tf_op jit(solution)/shard_map/ppermute | solution.py:84
  99.0 13.9 %collective-permute-start.23 = (bf16[128,2048]{1,0:T(8,128)(2,1)S(1)}, bf16[128,2048]{1,0:T(8,128)(2,1)}, u32[]{:S(2)}, u32[]{:S(2)}) collective-permute-start(bf16[128,2048]{1,0:T(8,128)(2,1)S(1)} %pad_maximum_fusion.4), channel_id=1, source_target_pairs={{0,2},{1,3},{2,0},{3,1},{4,6},{5,7},{6,4},{7,5},{8,10},{9,11},{10,... | collective-permute-start | bytes 1572872 | tf_op jit(solution)/shard_map/ppermute | solution.py:84
  99.6 17.1 %collective-permute-start.5 = (bf16[256,2048]{1,0:T(8,128)(2,1)}, bf16[256,2048]{1,0:T(8,128)(2,1)}, u32[]{:S(2)}, u32[]{:S(2)}) collective-permute-start(bf16[256,2048]{1,0:T(8,128)(2,1)} %get-tuple-element.21), channel_id=1, source_target_pairs={{0,1},{1,0},{2,3},{3,2},{4,5},{5,4},{6,7},{7,6},{8,9},{9,8},{10,11... | collective-permute-start | bytes 3145736 | tf_op jit(solution)/shard_map/ppermute | solution.py:84
  101.1 18.3 %collective-permute-start.33 = (bf16[128,2048]{1,0:T(8,128)(2,1)S(1)}, bf16[128,2048]{1,0:T(8,128)(2,1)S(1)}, u32[]{:S(2)}, u32[]{:S(2)}) collective-permute-start(bf16[128,2048]{1,0:T(8,128)(2,1)S(1)} %pad_maximum_fusion.5), channel_id=1, source_target_pairs={{0,4},{1,5},{2,6},{3,7},{4,0},{5,1},{6,2},{7,3},{8,12},{9,13},{10,... | collective-permute-start | bytes 1572872 | tf_op jit(solution)/shard_map/ppermute | solution.py:84
  116.1 12.9 %collective-permute-start.16 = (bf16[128,2048]{1,0:T(8,128)(2,1)S(1)}, bf16[128,2048]{1,0:T(8,128)(2,1)S(1)}, u32[]{:S(2)}, u32[]{:S(2)}) collective-permute-start(bf16[128,2048]{1,0:T(8,128)(2,1)S(1)} %slice.243), channel_id=1, source_target_pairs={{0,4},{1,5},{2,6},{3,7},{4,0},{5,1},{6,2},{7,3},{8,12},{9,13},{10,... | collective-permute-start | bytes 1572872 | tf_op jit(solution)/shard_map/ppermute | solution.py:84
  118.3 13.7 %collective-permute-start.6 = (bf16[128,2048]{1,0:T(8,128)(2,1)S(1)}, bf16[128,2048]{1,0:T(8,128)(2,1)S(1)}, u32[]{:S(2)}, u32[]{:S(2)}) collective-permute-start(bf16[128,2048]{1,0:T(8,128)(2,1)S(1)} %slice.231), channel_id=1, source_target_pairs={{0,2},{1,3},{2,0},{3,1},{4,6},{5,7},{6,4},{7,5},{8,10},{9,11},{10,... | collective-permute-start | bytes 1572872 | tf_op jit(solution)/shard_map/ppermute | solution.py:84
  119.5 17.5 %collective-permute-start.34 = (bf16[256,2048]{1,0:T(8,128)(2,1)S(1)}, bf16[256,2048]{1,0:T(8,128)(2,1)S(1)}, u32[]{:S(2)}, u32[]{:S(2)}) collective-permute-start(bf16[256,2048]{1,0:T(8,128)(2,1)S(1)} %pad_maximum_fusion.1.near_ref), channel_id=1, source_target_pairs={{0,1},{1,0},{2,3},{3,2},{4,5},{5,4},{6,7},{7,6},{8,9},{9,8},{10,11... | collective-permute-start | bytes 3145736 | tf_op jit(solution)/shard_map/ppermute | solution.py:84
  119.6 30.3 %collective-permute-start.24 = (bf16[256,2048]{1,0:T(8,128)(2,1)S(1)}, bf16[256,2048]{1,0:T(8,128)(2,1)S(1)}, u32[]{:S(2)}, u32[]{:S(2)}) collective-permute-start(bf16[256,2048]{1,0:T(8,128)(2,1)S(1)} %pad_maximum_fusion.near_ref), channel_id=1, source_target_pairs={{0,1},{1,0},{2,3},{3,2},{4,5},{5,4},{6,7},{7,6},{8,9},{9,8},{10,11... | collective-permute-start | bytes 3145736 | tf_op jit(solution)/shard_map/ppermute | solution.py:84
  129.1 7.5 %collective-permute-start.17 = (bf16[64,2048]{1,0:T(8,128)(2,1)S(1)}, bf16[64,2048]{1,0:T(8,128)(2,1)S(1)}, u32[]{:S(2)}, u32[]{:S(2)}) collective-permute-start(bf16[64,2048]{1,0:T(8,128)(2,1)S(1)} %slice.245), channel_id=1, source_target_pairs={{0,2},{1,3},{2,0},{3,1},{4,6},{5,7},{6,4},{7,5},{8,10},{9,11},{10,... | collective-permute-start | bytes 786440 | tf_op jit(solution)/shard_map/ppermute | solution.py:84
  132.2 31.1 %collective-permute-start.7 = (bf16[64,2048]{1,0:T(8,128)(2,1)S(1)}, bf16[64,2048]{1,0:T(8,128)(2,1)S(1)}, u32[]{:S(2)}, u32[]{:S(2)}) collective-permute-start(bf16[64,2048]{1,0:T(8,128)(2,1)S(1)} %slice.233), channel_id=1, source_target_pairs={{0,4},{1,5},{2,6},{3,7},{4,0},{5,1},{6,2},{7,3},{8,12},{9,13},{10,... | collective-permute-start | bytes 786440 | tf_op jit(solution)/shard_map/ppermute | solution.py:84
  136.7 28.4 %collective-permute-start.18 = (bf16[32,2048]{1,0:T(8,128)(2,1)S(1)}, bf16[32,2048]{1,0:T(8,128)(2,1)S(1)}, u32[]{:S(2)}, u32[]{:S(2)}) collective-permute-start(bf16[32,2048]{1,0:T(8,128)(2,1)S(1)} %slice.247), channel_id=1, source_target_pairs={{0,8},{1,9},{2,10},{3,11},{4,12},{5,13},{6,14},{7,15},{8,0},{9,1},... | collective-permute-start | bytes 393224 | tf_op jit(solution)/shard_map/ppermute | solution.py:84
  149.9 23.2 %collective-permute-start.35 = (bf16[256,2048]{1,0:T(8,128)(2,1)}, bf16[256,2048]{1,0:T(8,128)(2,1)S(1)}, u32[]{:S(2)}, u32[]{:S(2)}) collective-permute-start(bf16[256,2048]{1,0:T(8,128)(2,1)} %get-tuple-element.33), channel_id=1, source_target_pairs={{0,1},{1,0},{2,3},{3,2},{4,5},{5,4},{6,7},{7,6},{8,9},{9,8},{10,11... | collective-permute-start | bytes 3145736 | tf_op jit(solution)/shard_map/ppermute | solution.py:84
  162.7 12.3 %collective-permute-start.25 = (bf16[256,2048]{1,0:T(8,128)(2,1)}, bf16[256,2048]{1,0:T(8,128)(2,1)S(1)}, u32[]{:S(2)}, u32[]{:S(2)}) collective-permute-start(bf16[256,2048]{1,0:T(8,128)(2,1)} %get-tuple-element.28), channel_id=1, source_target_pairs={{0,1},{1,0},{2,3},{3,2},{4,5},{5,4},{6,7},{7,6},{8,9},{9,8},{10,11... | collective-permute-start | bytes 3145736 | tf_op jit(solution)/shard_map/ppermute | solution.py:84
  165.2 7.9 %collective-permute-start.19 = (bf16[16,2048]{1,0:T(8,128)(2,1)S(1)}, bf16[16,2048]{1,0:T(8,128)(2,1)S(1)}, u32[]{:S(2)}, u32[]{:S(2)}) collective-permute-start(bf16[16,2048]{1,0:T(8,128)(2,1)S(1)} %slice.249), channel_id=1, source_target_pairs={{0,16},{1,17},{2,18},{3,19},{4,20},{5,21},{6,22},{7,23},{8,24},{9,... | collective-permute-start | bytes 196616 | tf_op jit(solution)/shard_map/ppermute | solution.py:84
  173.5 12.1 %collective-permute-start.36 = (bf16[128,2048]{1,0:T(8,128)(2,1)S(1)}, bf16[128,2048]{1,0:T(8,128)(2,1)S(1)}, u32[]{:S(2)}, u32[]{:S(2)}) collective-permute-start(bf16[128,2048]{1,0:T(8,128)(2,1)S(1)} %slice.267), channel_id=1, source_target_pairs={{0,4},{1,5},{2,6},{3,7},{4,0},{5,1},{6,2},{7,3},{8,12},{9,13},{10,... | collective-permute-start | bytes 1572872 | tf_op jit(solution)/shard_map/ppermute | solution.py:84
  175.5 13.4 %collective-permute-start.26 = (bf16[128,2048]{1,0:T(8,128)(2,1)S(1)}, bf16[128,2048]{1,0:T(8,128)(2,1)S(1)}, u32[]{:S(2)}, u32[]{:S(2)}) collective-permute-start(bf16[128,2048]{1,0:T(8,128)(2,1)S(1)} %slice.255), channel_id=1, source_target_pairs={{0,2},{1,3},{2,0},{3,1},{4,6},{5,7},{6,4},{7,5},{8,10},{9,11},{10,... | collective-permute-start | bytes 1572872 | tf_op jit(solution)/shard_map/ppermute | solution.py:84
  185.8 7.2 %collective-permute-start.37 = (bf16[64,2048]{1,0:T(8,128)(2,1)S(1)}, bf16[64,2048]{1,0:T(8,128)(2,1)S(1)}, u32[]{:S(2)}, u32[]{:S(2)}) collective-permute-start(bf16[64,2048]{1,0:T(8,128)(2,1)S(1)} %slice.269), channel_id=1, source_target_pairs={{0,2},{1,3},{2,0},{3,1},{4,6},{5,7},{6,4},{7,5},{8,10},{9,11},{10,... | collective-permute-start | bytes 786440 | tf_op jit(solution)/shard_map/ppermute | solution.py:84
  (30 other events, 199.0 us)
